TPU v7x, 128 devices: a whole 4x4x4 slice. The times are simulated.
128 devices in a mesh: sub: 8 (over z, core), leaf: 16 (over y, x).
Axes of the slice: x: 4, y: 4, z: 4, core: 2. Of those that a mesh axis runs over, the one named last changes fastest.
Arguments:
- tiles: bfloat16 [512, 128, 128], replicated, may hold values from -0.5 to 0.5
- tile_rows: int32 [512], replicated, may hold values from 0 to 511, as said below
- tile_cols: int32 [512], replicated, may hold values from 0 to 1023
- cost: bfloat16 [512, 131072], P(('sub', 'leaf')), may hold values from -6 to 6
- demand: bfloat16 [512, 65536], P(('sub', 'leaf')), may hold values from -6 to 6
- upper: float32 [131072], replicated, may hold values from 0.5 to 4
- prob: float32 [512], P(('sub', 'leaf')), may hold values from 0.01 to 1
- node_of_scen: int32 [512], P(('sub', 'leaf')), may hold values from 0 to 127, as said below
- root_blocks: int32 [512], replicated, may hold values from 0 to 1023, as said below
- node_blocks: int32 [128, 128], replicated, may hold values from 0 to 1023, as said below
Outputs:
- primal: float32 [512, 131072], P(('sub', 'leaf'))
- dual: float32 [512, 65536], P(('sub', 'leaf'))
- multiplier: float32 [512, 131072], P(('sub', 'leaf'))
Inputs may be any that keep to these rules, and one draw needn't show every extreme that they name: `tile_rows`: each of the 512 row blocks is named by exactly 1 tiles. `node_of_scen`: scenario s belongs to a node of group g = (s // 4) % 16, numbered g * 8 to g * 8 + 7; every node has at least one scenario; node sizes are uneven. `root_blocks`: distinct block indices. `node_blocks`: each row holds 128 distinct block indices, none of them in root_blocks.
All inputs are finite; a program needn't handle non-finite values.
Results may differ from a plain program's by a relative error of at most 0.00088.
Values sent between devices are 32-bit elements; how exact they have to be, the bound alone decides.
A program may use at most 128 MiB of HBM per device.

v0:
```python
import jax
import jax.numpy as jnp
from jax import lax
from jax.sharding import PartitionSpec as P

PH_ITERS = 2
PD_STEPS = 2


primal_step = 1.0
dual_step = 0.25
penalty = 1.0


def select_blocks(select16, field16):
    count = field16.shape[0]
    width = select16.shape[1]
    shaped = field16.reshape(count, width, -1)
    picked = jnp.einsum("nv,svk->snk", select16, shaped, preferred_element_type=jnp.float32)
    return picked.astype(jnp.bfloat16)


def apply_matrix(tiles, col_select, row_select, field16):
    count = field16.shape[0]
    blocks = select_blocks(col_select, field16)
    terms = jnp.einsum("snk,nrk->nsr", blocks, tiles, preferred_element_type=jnp.float32)
    summed = jnp.einsum("nc,nsr->scr", row_select, terms, precision=lax.Precision.HIGHEST)
    return summed.reshape(count, -1)


def apply_transpose(tiles, row_select16, col_select, field16):
    count = field16.shape[0]
    blocks = select_blocks(row_select16, field16)
    terms = jnp.einsum("snr,nrk->nsk", blocks, tiles, preferred_element_type=jnp.float32)
    summed = jnp.einsum("nv,nsk->svk", col_select, terms, precision=lax.Precision.HIGHEST)
    return summed.reshape(count, -1)


def per_device(
    tiles, tile_rows, tile_cols, cost, demand, upper, prob, node_of_scen, root_blocks, node_blocks
):
    scen_count, var_count = cost.shape
    tile_width = tiles.shape[2]
    var_tiles = var_count // tile_width
    con_tiles = demand.shape[1] // tile_width
    per_group = node_blocks.shape[0] // lax.axis_size("leaf")
    group = lax.axis_index("leaf")
    row_match = tile_rows[:, None] == jnp.arange(con_tiles)[None, :]
    col_match = tile_cols[:, None] == jnp.arange(var_tiles)[None, :]
    row_select = row_match.astype(jnp.float32)
    row_select16 = row_match.astype(jnp.bfloat16)
    col_select = col_match.astype(jnp.float32)
    col_select16 = col_match.astype(jnp.bfloat16)
    local_node = node_of_scen - group * per_group
    onehot = (local_node[:, None] == jnp.arange(per_group)[None, :]).astype(jnp.float32)
    weighted = onehot * prob[:, None]
    group_weight = lax.psum(jnp.sum(weighted, axis=0), "sub")
    total_weight = lax.psum(jnp.sum(prob), ("sub", "leaf"))
    group_blocks = lax.dynamic_slice_in_dim(node_blocks, group * per_group, per_group, 0)
    own_blocks = jnp.dot(onehot, group_blocks.astype(jnp.float32), precision=lax.Precision.HIGHEST)
    root_select = (root_blocks[:, None] == jnp.arange(var_tiles)[None, :]).astype(jnp.float32)
    own_select = (
        own_blocks[:, :, None] == jnp.arange(var_tiles)[None, None, :].astype(jnp.float32)
    ).astype(jnp.float32)
    root_mask = jnp.sum(root_select, axis=0)
    block_mask = root_mask[None, :] + jnp.sum(own_select, axis=1) > 0.5
    cost_f = cost.astype(jnp.float32)
    demand_f = demand.astype(jnp.float32)
    primal = jnp.zeros((scen_count, var_count), jnp.float32)
    dual = jnp.zeros(demand.shape, jnp.float32)
    multiplier = jnp.zeros((scen_count, var_count), jnp.float32)
    consensus = jnp.zeros((scen_count, var_count), jnp.float32)
    for outer in range(PH_ITERS):
        for inner in range(PD_STEPS):
            gradient = apply_transpose(tiles, row_select16, col_select, dual.astype(jnp.bfloat16))
            moved = (
                primal
                - primal_step * (cost_f + multiplier - gradient)
                + primal_step * penalty * consensus
            )
            nextval = jnp.clip(moved / (1.0 + primal_step * penalty), 0.0, upper[None, :])
            extrap = (2.0 * nextval - primal).astype(jnp.bfloat16)
            image = apply_matrix(tiles, col_select16, row_select, extrap)
            dual = jnp.maximum(dual + dual_step * (demand_f - image), 0.0)
            primal = nextval
        shaped = primal.reshape(scen_count, var_tiles, tile_width)
        weighted_all = jnp.einsum("s,svt->vt", prob, shaped, precision=lax.Precision.HIGHEST)
        root_part = jnp.dot(root_select, weighted_all, precision=lax.Precision.HIGHEST)
        node_vals = jnp.einsum("sbv,svt->sbt", own_select, shaped, precision=lax.Precision.HIGHEST)
        node_part = jnp.einsum(
            "sn,sbt->nbt", weighted, node_vals, precision=lax.Precision.HIGHEST
        ).reshape(per_group, -1)
        root_mean = lax.psum(root_part, ("sub", "leaf")) / total_weight
        node_total = lax.psum(node_part, "sub")
        node_mean = node_total / group_weight[:, None]
        own_mean = jnp.dot(onehot, node_mean, precision=lax.Precision.HIGHEST).reshape(
            node_vals.shape
        )
        root_fill = jnp.dot(root_select.T, root_mean, precision=lax.Precision.HIGHEST)
        node_fill = jnp.einsum(
            "sbv,sbt->svt", own_select, own_mean, precision=lax.Precision.HIGHEST
        )
        merged = jnp.where(block_mask[:, :, None], root_fill[None, :, :] + node_fill, shaped)
        consensus = merged.reshape(scen_count, var_count)
        multiplier = multiplier + penalty * (primal - consensus)
    return (primal, dual, multiplier)


def solution(mesh):
    return jax.shard_map(
        per_device,
        mesh=mesh,
        in_specs=(
            P(),
            P(),
            P(),
            P(("sub", "leaf"), None),
            P(("sub", "leaf"), None),
            P(),
            P(("sub", "leaf")),
            P(("sub", "leaf")),
            P(),
            P(),
        ),
        out_specs=(P(("sub", "leaf"), None), P(("sub", "leaf"), None), P(("sub", "leaf"), None)),
        check_vma=False,
    )
```

profile of v0, /device:TPU:1, one launch (start us, length us, event | category | flops | bytes accessed | tf_op | source)
XLA Modules:
  0.0 582.2 jit_solution(13395802068484309823)
XLA Ops:
  7.2 1.3 fusion.87
  8.8 8.0 %fusion.215 = f32[512,4,128]{2,1,0:T(4,128)S(1)} fusion(bf16[4,512,128]{2,0,1:T(4,128)(2,1)S(1)} %copy.21, bf16[512,128,128]{2,1,0:T(8,128)(2,1)} %param.10), kind=kOutput, calls=%fused_computation.210 | convolution fusion | flops 67108864 | bytes 18350080 | tf_op jit(solution)/shard_map/snr,nrk->nsk/dot_general | solution.py:34
  16.9 3.4 fusion.59
  20.2 2.0 copy.23
  22.3 3.6 fusion.114
  25.9 1.7 fusion.100
  27.6 1.4 copy.25
  29.0 12.2 %fusion.216 = f32[512,4,128]{2,1,0:T(4,128)S(1)} fusion(bf16[4,512,128]{2,0,1:T(4,128)(2,1)S(1)} %copy.25, bf16[512,128,128]{2,1,0:T(8,128)(2,1)} %param.10), kind=kOutput, calls=%fused_computation.211 | convolution fusion | flops 67108864 | bytes 18350080 | tf_op jit(solution)/shard_map/snk,nrk->nsr/dot_general | solution.py:26
  41.2 2.2 convolution_bitcast_fusion.5
  43.4 1.5 copy.27
  46.8 8.2 %fusion.217 = f32[512,4,128]{2,1,0:T(4,128)S(1)} fusion(bf16[4,512,128]{2,0,1:T(4,128)(2,1)S(1)} %copy.29, bf16[512,128,128]{2,1,0:T(8,128)(2,1)} %param.10), kind=kOutput, calls=%fused_computation.212 | convolution fusion | flops 67108864 | bytes 18350080 | tf_op jit(solution)/shard_map/snr,nrk->nsk/dot_general | solution.py:34
  55.0 2.0 fusion.62
  57.0 1.8 copy.31
  58.8 7.1 %fusion.115 = (bf16[1,4,1024,128]{3,1,2,0:T(4,128)(2,1)}, f32[4,131072]{1,0:T(4,128)S(1)}) fusion(f32[1,4,1024,128]{3,2,1,0:T(8,128)} %bitcast.281, bf16[4,131072]{1,0:T(4,128)(2,1)S(1)} %copy-done.6, f32[131072]{0:T(1024)} %param.15, f32[1,4,1024,128]{3,2,1,0:T(8,128)} %bitcast.286), kind=kLoop, calls=%fused_computation.112 | loop fusion | flops 7340032 | bytes 8912896
  66.0 3.8 fusion.34
  69.8 1.8 fusion.39
  72.6 2.1 fusion.6
  74.7 1.7 convolution_bitcast_fusion.1
  78.3 2.9 fusion.97
  81.2 2.1 copy.35
  83.3 12.3 %fusion.218 = f32[512,4,128]{2,1,0:T(4,128)S(1)} fusion(bf16[4,512,128]{2,0,1:T(4,128)(2,1)} %copy.35, bf16[512,128,128]{2,1,0:T(8,128)(2,1)} %param.10), kind=kOutput, calls=%fused_computation.213 | convolution fusion | flops 67108864 | bytes 18350080 | tf_op jit(solution)/shard_map/snk,nrk->nsr/dot_general | solution.py:26
  95.7 2.2 convolution_bitcast_fusion.4
  97.8 2.5 copy.37
  100.4 4.3 convert_bitcast_fusion.1
  104.7 1.5 fusion.89
  106.1 2.1 copy.39
  108.3 8.2 %fusion.219 = f32[512,4,128]{2,1,0:T(4,128)S(1)} fusion(bf16[4,512,128]{2,0,1:T(4,128)(2,1)} %copy.39, bf16[512,128,128]{2,1,0:T(8,128)(2,1)} %param.10), kind=kOutput, calls=%fused_computation.214 | convolution fusion | flops 67108864 | bytes 18350080 | tf_op jit(solution)/shard_map/snr,nrk->nsk/dot_general | solution.py:34
  116.5 3.4 fusion.65
  119.8 69.8 %psum.43 = f32[]{:T(128)} all-reduce(f32[]{:T(128)} %reduce_sum.38), channel_id=1, replica_groups=mesh['sub'=8,'leaf'=16] {'sub','leaf'}, use_global_device_ids=true, to_apply=%region_4.0 | all-reduce | flops 1 | bytes 8 | tf_op jit(solution)/shard_map/psum | solution.py:58
  189.7 12.7 %psum.45 = f32[8]{0:T(128)S(1)} all-reduce(f32[8]{0:T(128)S(1)} %select_reduce_fusion), channel_id=1, replica_groups=mesh['sub'=8,'leaf'=16] {'sub'}, use_global_device_ids=true, to_apply=%region_7.8 | all-reduce | flops 8 | bytes 64 | tf_op jit(solution)/shard_map/psum | solution.py:57
  202.4 2.9 copy.41
  205.3 12.9 %all-reduce.5.cloned.1.call-done = f32[512,128]{1,0:T(8,128)} async-done(((f32[512,128]{1,0:T(8,128)}), f32[512,128]{1,0:T(8,128)}) %all-reduce.5.cloned.1.call-update) | async-done | bytes 262160 | tf_op jit(solution)/shard_map/psum | solution.py:93
  218.2 4.3 fusion.38
  222.5 54.7 %all-reduce.7.cloned.1.call-done = f32[8,16384]{1,0:T(8,128)} async-done(((f32[8,16384]{1,0:T(8,128)}), f32[8,16384]{1,0:T(8,128)}) %all-reduce.7.cloned.1.call-update) | async-done | bytes 524304 | tf_op jit(solution)/shard_map/psum | solution.py:94
  277.1 1.5 convolution_bitcast_fusion.7
  278.7 1.4 fusion.31
  280.4 6.6 %fusion.116 = bf16[1,4,1024,128]{3,1,2,0:T(4,128)(2,1)S(1)} fusion(f32[4,131072]{1,0:T(4,128)S(1)} %get-tuple-element.8, f32[1,4,1024,128]{3,2,1,0:T(8,128)S(1)} %bitcast.279, f32[1,4,1024,128]{3,2,1,0:T(8,128)S(1)} %fusion.31, bf16[4,131072]{1,0:T(4,128)(2,1)S(1)} %copy-done.6, f32[131072]{0:T(1024)S(1)} %copy-done.9), kind=kLoop, calls=%fused_computation.113 | loop fusion | flops 6291456 | bytes 8912896
  287.0 1.7 fusion.94
  288.7 2.1 copy.43
  290.8 12.5 %fusion.220 = f32[512,4,128]{2,1,0:T(4,128)S(1)} fusion(bf16[4,512,128]{2,0,1:T(4,128)(2,1)} %copy.43, bf16[512,128,128]{2,1,0:T(8,128)(2,1)} %param.10), kind=kOutput, calls=%fused_computation.215 | convolution fusion | flops 67108864 | bytes 18350080 | tf_op jit(solution)/shard_map/snk,nrk->nsr/dot_general | solution.py:26
  303.3 2.2 convolution_bitcast_fusion.3
  305.5 2.5 copy.45
  308.0 2.6 convert_bitcast_fusion
  310.6 1.5 fusion.90
  312.1 2.1 copy.47
  314.2 8.2 %fusion.221 = f32[512,4,128]{2,1,0:T(4,128)S(1)} fusion(bf16[4,512,128]{2,0,1:T(4,128)(2,1)} %copy.47, bf16[512,128,128]{2,1,0:T(8,128)(2,1)} %param.10), kind=kOutput, calls=%fused_computation.216 | convolution fusion | flops 67108864 | bytes 18350080 | tf_op jit(solution)/shard_map/snr,nrk->nsk/dot_general | solution.py:34
  322.4 3.4 fusion.68
  325.8 2.9 copy.49
  328.6 9.9 %fusion.117 = (bf16[1,4,1024,128]{3,1,2,0:T(4,128)(2,1)S(1)}, f32[4,131072]{1,0:T(4,128)}) fusion(f32[4,131072]{1,0:T(4,128)S(1)} %get-tuple-element.8, f32[1,4,1024,128]{3,2,1,0:T(8,128)} %bitcast.278, f32[1,4,1024,128]{3,2,1,0:T(8,128)} %copy-done.2, bf16[4,131072]{1,0:T(4,128)(2,1)S(1)} %copy-done.6, f32[131072]{0:T(1024)} %param.15, ...), kind=kLoop, calls=%fused_computation.114 | loop fusion | flops 9437184 | bytes 13107200
  339.4 1.1 copy.51
  340.5 5.4 fusion.32
  346.0 2.1 fusion.2
  348.0 12.2 %fusion.222 = f32[512,4,128]{2,1,0:T(4,128)S(1)} fusion(bf16[4,512,128]{2,0,1:T(4,128)(2,1)S(1)} %copy-done.11, bf16[512,128,128]{2,1,0:T(8,128)(2,1)} %param.10), kind=kOutput, calls=%fused_computation.217 | convolution fusion | flops 67108864 | bytes 18350080 | tf_op jit(solution)/shard_map/snk,nrk->nsr/dot_general | solution.py:26
  360.2 1.8 fusion.37
  362.4 2.2 convolution_bitcast_fusion.2
  364.6 2.6 copy.53
  367.2 1.6 convolution_bitcast_fusion
  368.9 4.3 fusion.113
  373.2 133.3 %all-reduce.9.cloned.1.call-done = f32[512,128]{1,0:T(8,128)} async-done(((f32[512,128]{1,0:T(8,128)}), f32[512,128]{1,0:T(8,128)}) %all-reduce.9.cloned.1.call-update) | async-done | bytes 262160 | tf_op jit(solution)/shard_map/psum | solution.py:93
  506.5 3.5 fusion.36
  509.9 55.3 %all-reduce.11.cloned.1.call-done = f32[8,16384]{1,0:T(8,128)} async-done(((f32[8,16384]{1,0:T(8,128)}), f32[8,16384]{1,0:T(8,128)}) %all-reduce.11.cloned.1.call-update) | async-done | bytes 524304 | tf_op jit(solution)/shard_map/psum | solution.py:94
  565.3 1.5 convolution_bitcast_fusion.6
  566.8 4.1 fusion.19
  570.9 4.3 fusion.17
  (57 shorter events, 6.6 us)
Async XLA Ops:
  7.2 211.0 %all-reduce.5.cloned.1.call-start = ((), (), s32[]{:S(2)}) async-start(), calls=%async_computation | async-start | bytes 524288 | tf_op jit(solution)/shard_map/psum | solution.py:93
  8.8 8.1 %copy-start.14 = (s32[512]{0:T(512)S(1)}, s32[512]{0:T(512)}, u32[]{:S(2)}) copy-start(s32[512]{0:T(512)} %param.12) | copy-start | bytes 6148
  20.2 2.0 copy-start.6
  22.2 3.6 copy-start.5
  28.9 12.2 %copy-start.13 = (s32[512]{0:T(512)S(1)}, s32[512]{0:T(512)}, u32[]{:S(2)}) copy-start(s32[512]{0:T(512)} %param.11) | copy-start | bytes 6148
  41.2 3.8 copy-start.10
  44.9 1.8 copy-start.8
  58.8 7.1 %copy-start.15 = (f32[4]{0:T(128)S(1)}, f32[4]{0:T(128)}, u32[]{:S(2)}) copy-start(f32[4]{0:T(128)} %param.16) | copy-start | bytes 52
  66.0 3.9 copy-start.16
  66.0 5.8 copy-start.17
  71.7 205.5 %all-reduce.7.cloned.1.call-start = ((), (), s32[]{:S(2)}) async-start(), calls=%async_computation.1 | async-start | bytes 1048576 | tf_op jit(solution)/shard_map/psum | solution.py:94
  76.4 430.1 %all-reduce.9.cloned.1.call-start = ((), (), s32[]{:S(2)}) async-start(), calls=%async_computation.2 | async-start | bytes 524288 | tf_op jit(solution)/shard_map/psum | solution.py:93
  277.1 1.6 copy-start.12
  278.7 1.6 copy-start.4
  278.7 1.7 copy-start.9
  280.1 6.9 %copy-start.2 = (f32[1,4,1024,128]{3,2,1,0:T(8,128)}, f32[1,4,1024,128]{3,2,1,0:T(8,128)S(1)}, u32[]{:S(2)}) copy-start(f32[1,4,1024,128]{3,2,1,0:T(8,128)S(1)} %fusion.31) | copy-start | bytes 6291460
  340.5 5.5 copy-start
  340.5 7.5 %copy-start.11 = (bf16[4,512,128]{2,0,1:T(4,128)(2,1)S(1)}, bf16[4,512,128]{2,0,1:T(4,128)(2,1)}, u32[]{:S(2)}) copy-start(bf16[4,512,128]{2,0,1:T(4,128)(2,1)} %copy.51) | copy-start | bytes 1572868
  362.1 203.2 %all-reduce.11.cloned.1.call-start = ((), (), s32[]{:S(2)}) async-start(), calls=%async_computation.3 | async-start | bytes 1048576 | tf_op jit(solution)/shard_map/psum | solution.py:94
  364.6 4.3 copy-start.7
  566.8 4.1 copy-start.1
  566.8 4.1 copy-start.3
Sparse Core Ops, SparseCore 0:
  71.8 146.3 all-reduce.4
  220.5 56.5 all-reduce.6
  362.2 144.1 all-reduce.8
  508.7 56.5 all-reduce.10
where the time goes:
time: 594 us; the launch traced here: 582 us
  waiting for transfers between devices  256 us (43%)
  matrix products  152 us (26%)
  blocking collectives  82.6 us (14%)
  other arithmetic  45.1 us (8%)
  local copies, waits for them, and re-layouts  30.6 us (5%)
  between operations  14.6 us (2%)
    psum x2, waiting for transfers between devices, per_device(): root_mean = lax.psum(root_part, ('sub', 'leaf')) / total_weight  146 us
    psum x2, waiting for transfers between devices, per_device(): node_total = lax.psum(node_part, 'sub')  110 us
    psum x1, blocking collectives, per_device(): total_weight = lax.psum(jnp.sum(prob), ('sub', 'leaf'))  69.8 us
    dot_general x4, matrix products, apply_matrix(): jnp.einsum('snk,nrk->nsr', blocks, tiles, preferred_element_type=jnp.floa...  49.2 us
    unnamed x7, other arithmetic  34.9 us
    dot_general x4, matrix products, apply_transpose(): jnp.einsum('snr,nrk->nsk', blocks, tiles, preferred_element_type=jnp.floa...  32.7 us
    psum x1, blocking collectives, per_device(): group_weight = lax.psum(jnp.sum(weighted, axis=0), 'sub')  12.7 us
    dot_general x8, matrix products, select_blocks(): jnp.einsum('nv,svk->snk', select16, shaped, preferred_element_type=jnp.fl...  12.2 us
  transfers between devices with their start and end apart: 4, of which 4 were waited for; matrix products, arithmetic and copies ran while one was open for 12% of the time, Pallas kernels for 0%

commit v1 on v0

v1 whole, which is shorter than its diff:
```python
import functools

import jax
import jax.numpy as jnp
from jax import lax
from jax.experimental import pallas as pl
from jax.experimental.pallas import tpu as pltpu
from jax.sharding import PartitionSpec as P

F32 = jnp.float32
BF16 = jnp.bfloat16
MESH = pl.DeviceIdType.MESH
LANES = 128
PAD = 8


def aligned(value, step=8):
    return pl.multiple_of(value, step)


def top_rows():
    return lax.broadcasted_iota(jnp.int32, (8, LANES), 0) < 4


def unroll_of(count, most):
    step = min(count, most)
    while count % step:
        step -= 1
    return step


def loop(count, most, body, carry=0):
    step = unroll_of(count, most)

    def outer(i, state):
        for u in range(step):
            state = body(i * step + u, state)
        return state

    return lax.fori_loop(0, count // step, outer, carry)


def start_tiles(tiles_hbm, tiles, sems, chunks):
    size = tiles.shape[0] // chunks
    for c in range(chunks):
        part = pl.ds(c * size, size)
        pltpu.make_async_copy(tiles_hbm.at[part], tiles.at[part], sems.at[c]).start()


def wait_tiles(tiles_hbm, tiles, sems, chunks, c):
    size = tiles.shape[0] // chunks
    part = pl.ds(c * size, size)
    pltpu.make_async_copy(tiles_hbm.at[part], tiles.at[part], sems.at[c]).wait()


def pick_pair(ref, first4, second4):
    low = ref[pl.ds(first4 + PAD, 8), :]
    high = ref[pl.ds(second4 + (PAD - 4), 8), :]
    return jnp.where(top_rows(), low, high)


def spread_upper(upper, wide):
    blocks = upper.shape[0]
    for s in range(4):
        wide[pl.ds(s, blocks, stride=4), :] = upper[...]


def pairs_a(tiles, cols4, field, pairs, emit, most):
    def body(p, state):
        lhs = pick_pair(field, cols4[2 * p], cols4[2 * p + 1]).astype(BF16)
        rhs = tiles[pl.ds(2 * p, 2)].reshape(2 * LANES, LANES)
        both = lax.dot_general(lhs, rhs, (((1,), (1,)), ((), ())), preferred_element_type=F32)
        emit(p, jnp.where(top_rows(), both[:, :LANES], both[:, LANES:]))
        return state

    first, count = pairs
    step = unroll_of(count, most)

    def outer(i, state):
        for u in range(step):
            body(first + i * step + u, state)
        return state

    lax.fori_loop(0, count // step, outer, 0)


def transpose_pass(tiles, order, order4, follows, dual, sums, most):
    pairs = tiles.shape[0] // 2
    zero = jnp.zeros((8, LANES), F32)
    sums[pl.ds(PAD + 8 * pairs, 8), :] = zero

    def body(p, carry):
        a, b = 2 * p, 2 * p + 1
        top = top_rows()
        low = dual[pl.ds(order4[a] + PAD, 8), :]
        high = dual[pl.ds(order4[b] + (PAD - 4), 8), :]
        lhs = jnp.concatenate([jnp.where(top, low, 0.0), jnp.where(top, 0.0, high)], axis=1)
        rhs = jnp.concatenate([tiles[order[a]], tiles[order[b]]], axis=0)
        own = lax.dot_general(
            lhs.astype(BF16), rhs, (((1,), (0,)), ((), ())), preferred_element_type=F32
        )
        fa, fb = follows[a], follows[b]
        other = pltpu.roll(own, 4, 0)
        within = own + jnp.where(top, 0.0, fb) * other
        full = jnp.where(top, fb * own + other, within)
        both = fa * fb
        sums[pl.ds(aligned(PAD + 8 * p), 8), :] = within + jnp.where(top, fa, both) * carry
        return both * carry + full

    loop(pairs, most, body, zero)


def first_step(cost, wide, field):
    rows = cost.shape[0]

    def body(i, state):
        at = aligned(16 * i, 16)
        moved = -cost[pl.ds(at, 16), :].astype(F32) * 0.5
        field[pl.ds(at + PAD, 16), :] = 2.0 * jnp.clip(moved, 0.0, wide[pl.ds(at, 16), :])
        return state

    loop(rows // 16, 8, body)


def later_step(cost, wide, sums, last4, base, primal_out, field, old):
    rows = cost.shape[0]

    def body(i, state):
        at = aligned(16 * i, 16)
        gradient = jnp.concatenate(
            [
                pick_pair(sums, last4[4 * i], last4[4 * i + 1]),
                pick_pair(sums, last4[4 * i + 2], last4[4 * i + 3]),
            ],
            axis=0,
        )
        before = old(at)
        moved = base(at, before) - cost[pl.ds(at, 16), :].astype(F32) + gradient
        after = jnp.clip(moved * 0.5, 0.0, wide[pl.ds(at, 16), :])
        primal_out[pl.ds(at, 16), :] = after
        field[pl.ds(at + PAD, 16), :] = 2.0 * after - before
        return state

    loop(rows // 16, 8, body)


def weigh(primal, prob, node_of, root_blocks, node_blocks, group, total, vals, root_part, node_part):
    blocks = total.shape[0]
    acc = prob[0] * primal[pl.ds(0, blocks, stride=4), :]
    for s in range(1, 4):
        acc = acc + prob[s] * primal[pl.ds(s, blocks, stride=4), :]
    total[...] = acc

    root_count = root_blocks.shape[0]
    pieces = (root_part.shape[0] - root_count) // 8
    each = root_count // pieces
    split = each + 8

    def root_body(i, state):
        for u in range(each):
            row = total[pl.ds(root_blocks[i * each + u], 1), :]
            root_part[pl.ds(i * split + u, 1), :] = row
        weight = prob[0] + prob[1] + prob[2] + prob[3]
        root_part[pl.ds(i * split + each, 8), :] = jnp.full((8, LANES), weight, F32)
        return state

    lax.fori_loop(0, pieces, root_body, 0)

    width = node_blocks.shape[1]
    for s in range(4):

        def node_body(b, state):
            row = primal[pl.ds(4 * node_blocks[node_of[s], b] + s, 1), :]
            vals[pl.ds(s * width + b, 1), :] = row
            return state

        loop(width, 16, node_body)

    nodes = node_part.shape[0] // (width + 8)
    for m in range(nodes):
        slot = (m % 2) * (nodes // 2) + m // 2
        share = [
            jnp.where(node_of[s] == group * nodes + m, prob[s], 0.0) for s in range(4)
        ]
        part = share[0] * vals[pl.ds(0, width), :]
        for s in range(1, 4):
            part = part + share[s] * vals[pl.ds(s * width, width), :]
        node_part[pl.ds(slot * (width + 8), width), :] = part
        node_part[pl.ds(slot * (width + 8) + width, 8), :] = jnp.full(
            (8, LANES), share[0] + share[1] + share[2] + share[3], F32
        )


def split_two(value):
    high = value.astype(BF16)
    low = (value - high.astype(F32)).astype(BF16)
    return jnp.concatenate([high, low], axis=1)


def fill_means(root_mean, node_mean, root_row, node_row, node_of, group, filled, mask):
    blocks = filled.shape[0] // 4
    chunk = min(blocks, 256)
    width = node_mean.shape[0] // 8
    ones_root = jnp.ones((root_mean.shape[0], LANES), BF16)
    ones_node = jnp.ones((width, LANES), BF16)
    root_rhs = split_two(root_mean[...])
    node_rhs = []
    for s in range(4):
        m = node_of[s] - group * 8
        slot = (m % 2) * 4 + m // 2
        node_rhs.append(split_two(node_mean[pl.ds(aligned(slot * width), width), :]))
    for i in range(blocks // chunk):
        here = lax.broadcasted_iota(jnp.int32, (chunk, root_row.shape[1]), 0) + i * chunk
        hot = (here == root_row[...]).astype(F32).astype(BF16)
        got = jnp.dot(hot, root_rhs, preferred_element_type=F32)
        root_fill = got[:, :LANES] + got[:, LANES:]
        root_mask = jnp.dot(hot, ones_root, preferred_element_type=F32)
        here = lax.broadcasted_iota(jnp.int32, (chunk, width), 0) + i * chunk
        for s in range(4):
            hot = (here == node_row[pl.ds(node_of[s], 1), :]).astype(F32).astype(BF16)
            got = jnp.dot(hot, node_rhs[s], preferred_element_type=F32)
            rows = pl.ds(4 * i * chunk + s, chunk, stride=4)
            filled[rows, :] = root_fill + got[:, :LANES] + got[:, LANES:]
            mask[rows, :] = root_mask + jnp.dot(hot, ones_node, preferred_element_type=F32)


def first_kernel(
    chunks, most,
    cols4, rows4, order, order4, follows, last4, prob, node_of, root_blocks, node_blocks,
    tiles_hbm, cost, demand, upper,
    primal_out, dual_out, sums_out, demand_out, wide_out, root_part, node_part,
    tiles, field, total, vals, demand_f, sems,
):
    group = lax.axis_index("leaf")
    start_tiles(tiles_hbm, tiles, sems, chunks)
    spread_upper(upper, wide_out)
    demand_f[pl.ds(PAD, demand.shape[0]), :] = demand[...].astype(F32)
    first_step(cost, wide_out, field)
    pairs = tiles.shape[0] // 2
    per_chunk = pairs // chunks

    def emit_first(p, image):
        want = pick_pair(demand_f, rows4[2 * p], rows4[2 * p + 1])
        demand_out[pl.ds(aligned(8 * p), 8), :] = want
        dual_out[pl.ds(aligned(PAD + 8 * p), 8), :] = jnp.maximum(0.25 * (want - image), 0.0)

    def chunk_body(c, state):
        wait_tiles(tiles_hbm, tiles, sems, chunks, c)
        pairs_a(tiles, cols4, field, (c * per_chunk, per_chunk), emit_first, most)
        return state

    lax.fori_loop(0, chunks, chunk_body, 0)
    transpose_pass(tiles, order, order4, follows, dual_out, sums_out, most)
    later_step(
        cost, wide_out, sums_out, last4,
        lambda at, before: before, primal_out, field,
        lambda at: 0.5 * field[pl.ds(at + PAD, 16), :],
    )
    weigh(primal_out, prob, node_of, root_blocks, node_blocks, group, total, vals, root_part, node_part)

    def emit_next(p, image):
        at = aligned(8 * p)
        old = dual_out[pl.ds(at + PAD, 8), :]
        dual_out[pl.ds(at + PAD, 8), :] = jnp.maximum(
            old + 0.25 * (demand_out[pl.ds(at, 8), :] - image), 0.0
        )

    pairs_a(tiles, cols4, field, (0, pairs), emit_next, most)
    transpose_pass(tiles, order, order4, follows, dual_out, sums_out, most)


def second_kernel(
    chunks, most,
    cols4, order, order4, follows, last4, inverse4, prob, node_of, root_blocks, node_blocks,
    tiles_hbm, cost, wide, demand_n, primal_in, dual_in, sums, root_mean, node_mean, root_row, node_row,
    primal_out, dual_final, rest_out, root_part, node_part,
    tiles, field, total, vals, dual, sums_next, filled, mask, third, sems,
):
    group = lax.axis_index("leaf")
    start_tiles(tiles_hbm, tiles, sems, chunks)
    fill_means(root_mean, node_mean, root_row, node_row, node_of, group, filled, mask)
    rows = primal_in.shape[0]
    pairs = tiles.shape[0] // 2
    per_chunk = pairs // chunks

    def consensus(at, before):
        return jnp.where(mask[pl.ds(at, 16), :] > 0.5, filled[pl.ds(at, 16), :], before)

    later_step(
        cost, wide, sums, last4,
        lambda at, before: 2.0 * consensus(at, before), third, field,
        lambda at: primal_in[pl.ds(at, 16), :],
    )

    def emit(source):
        def run(p, image):
            at = aligned(8 * p)
            old = source[pl.ds(at + PAD, 8), :]
            dual[pl.ds(at + PAD, 8), :] = jnp.maximum(
                old + 0.25 * (demand_n[pl.ds(at, 8), :] - image), 0.0
            )

        return run

    def chunk_body(c, state):
        wait_tiles(tiles_hbm, tiles, sems, chunks, c)
        pairs_a(tiles, cols4, field, (c * per_chunk, per_chunk), emit(dual_in), most)
        return state

    lax.fori_loop(0, chunks, chunk_body, 0)
    transpose_pass(tiles, order, order4, follows, dual, sums_next, most)

    def pull(at, before):
        start = primal_in[pl.ds(at, 16), :]
        middle = consensus(at, start)
        return before - (start - middle) + middle

    later_step(
        cost, wide, sums_next, last4, pull, primal_out, field,
        lambda at: third[pl.ds(at, 16), :],
    )
    weigh(primal_out, prob, node_of, root_blocks, node_blocks, group, total, vals, root_part, node_part)

    def rest_body(i, state):
        at = aligned(16 * i, 16)
        start = primal_in[pl.ds(at, 16), :]
        rest_out[pl.ds(at, 16), :] = (
            start - consensus(at, start) + primal_out[pl.ds(at, 16), :]
        )
        return state

    loop(rows // 16, 8, rest_body)
    pairs_a(tiles, cols4, field, (0, pairs), emit(dual), most)

    def order_body(r, state):
        dual_final[pl.ds(aligned(8 * r), 8), :] = pick_pair(
            dual, inverse4[2 * r], inverse4[2 * r + 1]
        )
        return state

    loop(pairs, 16, order_body)


def last_kernel(node_of, rest, root_mean, node_mean, root_row, node_row, multiplier, filled, mask):
    group = lax.axis_index("leaf")
    fill_means(root_mean, node_mean, root_row, node_row, node_of, group, filled, mask)

    def body(i, state):
        at = aligned(16 * i, 16)
        left = rest[pl.ds(at, 16), :] - filled[pl.ds(at, 16), :]
        multiplier[pl.ds(at, 16), :] = jnp.where(mask[pl.ds(at, 16), :] > 0.5, left, 0.0)
        return state

    loop(rest.shape[0] // 16, 8, body)


def wait_bytes(ref, sem):
    pltpu.make_async_copy(ref, ref, sem).wait()


def comm_kernel(
    ny, nx, nz, root_part, node_part, root_out, node_out,
    r0, n0, rsum, nsum, r1, n1, rz, r2, root_all, node_all, send, recv,
):
    sub, leaf = lax.axis_index("sub"), lax.axis_index("leaf")
    z, core = sub // 2, sub % 2
    y, x = leaf // nx, leaf % nx
    cells = ny * nx
    chunk = r1.shape[0] // max(cells - 1, 1)
    keep = chunk - 8
    rows = nsum.shape[0] // nz
    width = rows - 8
    half_r, half_n = cells * chunk, nz * rows

    partner = {"sub": z * 2 + (1 - core), "leaf": leaf}
    plane = []
    for k in range(1, cells):
        ky, kx = k // nx, k % nx
        other = ((y + ky) % ny) * nx + (x + kx) % nx
        plane.append((k, other, {"sub": sub, "leaf": other}))
    column = []
    for k in range(1, nz):
        other = (z + k) % nz
        column.append((k, other, {"sub": other * 2 + core, "leaf": leaf}))

    barrier = pltpu.get_barrier_semaphore()
    peers = [partner] + [p[2] for p in plane] + [p[2] for p in column]
    for peer in peers:
        pl.semaphore_signal(barrier, inc=1, device_id=peer, device_id_type=MESH)
    pl.semaphore_wait(barrier, len(peers))

    def push(src, dst, which, peer):
        pltpu.make_async_remote_copy(
            src_ref=src, dst_ref=dst, send_sem=send.at[which], recv_sem=recv.at[which],
            device_id=peer, device_id_type=MESH,
        ).start()

    push(node_part.at[pl.ds(aligned((1 - core) * half_n), half_n)], n0, 0, partner)
    push(root_part.at[pl.ds(aligned((1 - core) * half_r), half_r)], r0, 1, partner)
    wait_bytes(n0, recv.at[0])
    nsum[...] = node_part[pl.ds(aligned(core * half_n), half_n), :] + n0[...]
    for k, other, peer in column:
        push(
            nsum.at[pl.ds(aligned(other * rows), rows)],
            n1.at[pl.ds((k - 1) * rows, rows)], 2, peer,
        )
    wait_bytes(r0, recv.at[1])
    rsum[...] = root_part[pl.ds(aligned(core * half_r), half_r), :] + r0[...]
    for k, other, peer in plane:
        push(
            rsum.at[pl.ds(aligned(other * chunk), chunk)],
            r1.at[pl.ds((k - 1) * chunk, chunk)], 3, peer,
        )
    if nz > 1:
        wait_bytes(n1, recv.at[2])
    acc = nsum[pl.ds(aligned(z * rows), rows), :]
    for k in range(1, nz):
        acc = acc + n1[pl.ds((k - 1) * rows, rows), :]
    mine = (core * nz + z) * width
    node_all[pl.ds(aligned(mine), width), :] = acc[:width] / acc[width:width + 1]
    for k, other, peer in column:
        spot = node_all.at[pl.ds(aligned(mine), width)]
        push(spot, spot, 4, peer)
    if cells > 1:
        wait_bytes(r1, recv.at[3])
    acc = rsum[pl.ds(aligned(leaf * chunk), chunk), :]
    for k in range(1, cells):
        acc = acc + r1[pl.ds((k - 1) * chunk, chunk), :]
    rz[...] = acc
    for k, other, peer in column:
        push(rz, r2.at[pl.ds((k - 1) * chunk, chunk)], 5, peer)
    if nz > 1:
        wait_bytes(node_all.at[pl.ds(0, (nz - 1) * width)], recv.at[4])
    spot = node_all.at[pl.ds(aligned(core * nz * width), nz * width)]
    push(spot, spot, 6, partner)
    if nz > 1:
        wait_bytes(r2, recv.at[5])
    total = rz[...]
    for k in range(1, nz):
        total = total + r2[pl.ds((k - 1) * chunk, chunk), :]
    mine = (core * cells + leaf) * keep
    root_all[pl.ds(aligned(mine), keep), :] = total[:keep] / total[keep:keep + 1]
    for k, other, peer in plane:
        spot = root_all.at[pl.ds(aligned(mine), keep)]
        push(spot, spot, 7, peer)
    if cells > 1:
        wait_bytes(root_all.at[pl.ds(0, (cells - 1) * keep)], recv.at[7])
    spot = root_all.at[pl.ds(aligned(core * cells * keep), cells * keep)]
    push(spot, spot, 8, partner)
    wait_bytes(node_all.at[pl.ds(0, nz * width)], recv.at[6])
    node_out[...] = node_all[...]
    wait_bytes(root_all.at[pl.ds(0, cells * keep)], recv.at[8])
    root_out[...] = root_all[...]
    wait_bytes(n0, send.at[0])
    wait_bytes(r0, send.at[1])
    if nz > 1:
        wait_bytes(n1, send.at[2])
        wait_bytes(node_all.at[pl.ds(0, (nz - 1) * width)], send.at[4])
        wait_bytes(r2, send.at[5])
    if cells > 1:
        wait_bytes(r1, send.at[3])
        wait_bytes(root_all.at[pl.ds(0, (cells - 1) * keep)], send.at[7])
    wait_bytes(node_all.at[pl.ds(0, nz * width)], send.at[6])
    wait_bytes(root_all.at[pl.ds(0, cells * keep)], send.at[8])


def comm(root_part, node_part, root_count, width):
    leaf, sub = lax.axis_size("leaf"), lax.axis_size("sub")
    nz = sub // 2
    ny = 4 if leaf == 16 else 1
    nx = leaf // ny
    chunk = root_part.shape[0] // (2 * leaf)
    rows = width + 8
    vm = functools.partial(pltpu.VMEM, dtype=F32)
    return pl.pallas_call(
        functools.partial(comm_kernel, ny, nx, nz),
        out_shape=[
            jax.ShapeDtypeStruct((root_count, LANES), F32),
            jax.ShapeDtypeStruct((8 * width, LANES), F32),
        ],
        in_specs=[pl.BlockSpec(memory_space=pltpu.VMEM)] * 2,
        out_specs=[pl.BlockSpec(memory_space=pltpu.VMEM)] * 2,
        scratch_shapes=[
            vm((leaf * chunk, LANES)),
            vm((nz * rows, LANES)),
            vm((leaf * chunk, LANES)),
            vm((nz * rows, LANES)),
            vm(((leaf - 1) * chunk, LANES)),
            vm((max(nz - 1, 1) * rows, LANES)),
            vm((chunk, LANES)),
            vm((max(nz - 1, 1) * chunk, LANES)),
            vm((root_count, LANES)),
            vm((8 * width, LANES)),
            pltpu.SemaphoreType.DMA((9,)),
            pltpu.SemaphoreType.DMA((9,)),
        ],
        compiler_params=pltpu.CompilerParams(collective_id=0, has_side_effects=True),
        name="mean_exchange",
    )(root_part, node_part)


def as_rows(field):
    count, size = field.shape
    return field.reshape(count, size // LANES, LANES).transpose(1, 0, 2).reshape(-1, LANES)


def from_rows(rows):
    blocks = rows.shape[0] // 4
    return rows.reshape(blocks, 4, LANES).transpose(1, 0, 2).reshape(4, blocks * LANES)


def per_device(
    tiles, tile_rows, tile_cols, cost, demand, upper, prob, node_of_scen, root_blocks, node_blocks
):
    nt = tiles.shape[0]
    nvt = cost.shape[1] // LANES
    nct = demand.shape[1] // LANES
    width = node_blocks.shape[1]
    root_count = root_blocks.shape[0]
    leaf = lax.axis_size("leaf")
    chunks = 8
    most = 32
    with jax.named_scope("tables"):
        n = jnp.arange(nt, dtype=jnp.int32)
        ahead = (tile_cols[None, :] < tile_cols[:, None]) | (
            (tile_cols[None, :] == tile_cols[:, None]) & (n[None, :] < n[:, None])
        )
        rank = jnp.sum(ahead.astype(jnp.int32), axis=1)
        place = rank[None, :] == n[:, None]
        order = jnp.sum(jnp.where(place, n[None, :], 0), axis=1)
        sorted_col = jnp.sum(jnp.where(place, tile_cols[None, :], 0), axis=1)
        follows = jnp.concatenate(
            [jnp.zeros((1,), F32), (sorted_col[1:] == sorted_col[:-1]).astype(F32)]
        )
        v = jnp.arange(nvt, dtype=jnp.int32)
        upto = jnp.sum((tile_cols[None, :] <= v[:, None]).astype(jnp.int32), axis=1)
        has = jnp.sum((tile_cols[None, :] == v[:, None]).astype(jnp.int32), axis=1)
        last4 = 4 * jnp.where(has > 0, upto - 1, nt)
        inverse4 = 4 * jnp.sum(
            jnp.where(tile_rows[None, :] == jnp.arange(nct)[:, None], n[None, :], 0), axis=1
        )
        cols4, rows4, order4 = 4 * tile_cols, 4 * tile_rows, 4 * order
    cost_r, demand_r = as_rows(cost), as_rows(demand)
    upper_r = upper.reshape(nvt, LANES)
    root_row = root_blocks.reshape(1, root_count)
    part_rows = 2 * leaf * (root_count // (2 * leaf) + 8)
    sm = pl.BlockSpec(memory_space=pltpu.SMEM)
    vm = pl.BlockSpec(memory_space=pltpu.VMEM)
    hbm = pl.BlockSpec(memory_space=pl.ANY)
    shape = jax.ShapeDtypeStruct
    params = pltpu.CompilerParams(vmem_limit_bytes=62 * 1024 * 1024)
    pad_rows = PAD + 4 * nt + 16
    state_rows = 4 * nvt
    primal2, dual2, sums2, demand_n, wide, root_part, node_part = pl.pallas_call(
        functools.partial(first_kernel, chunks, most),
        out_shape=[
            shape((state_rows, LANES), F32),
            shape((pad_rows, LANES), F32),
            shape((pad_rows, LANES), F32),
            shape((4 * nt, LANES), F32),
            shape((state_rows, LANES), F32),
            shape((part_rows, LANES), F32),
            shape((8 * (width + 8), LANES), F32),
        ],
        in_specs=[sm] * 10 + [hbm, vm, vm, vm],
        out_specs=[vm] * 7,
        scratch_shapes=[
            pltpu.VMEM(tiles.shape, BF16),
            pltpu.VMEM((state_rows + 2 * PAD, LANES), F32),
            pltpu.VMEM((nvt, LANES), F32),
            pltpu.VMEM((4 * width, LANES), F32),
            pltpu.VMEM((4 * nct + 2 * PAD, LANES), F32),
            pltpu.SemaphoreType.DMA((chunks,)),
        ],
        compiler_params=params,
        name="first_iteration",
    )(
        cols4, rows4, order, order4, follows, last4, prob, node_of_scen, root_blocks, node_blocks,
        tiles, cost_r, demand_r, upper_r,
    )
    root_mean, node_mean = comm(root_part, node_part, root_count, width)
    primal, dual, rest, root_part, node_part = pl.pallas_call(
        functools.partial(second_kernel, chunks, most),
        out_shape=[
            shape((state_rows, LANES), F32),
            shape((4 * nct, LANES), F32),
            shape((state_rows, LANES), F32),
            shape((part_rows, LANES), F32),
            shape((8 * (width + 8), LANES), F32),
        ],
        in_specs=[sm] * 10 + [hbm] + [vm] * 10,
        out_specs=[vm] * 5,
        scratch_shapes=[
            pltpu.VMEM(tiles.shape, BF16),
            pltpu.VMEM((state_rows + 2 * PAD, LANES), F32),
            pltpu.VMEM((nvt, LANES), F32),
            pltpu.VMEM((4 * width, LANES), F32),
            pltpu.VMEM((pad_rows, LANES), F32),
            pltpu.VMEM((pad_rows, LANES), F32),
            pltpu.VMEM((state_rows, LANES), F32),
            pltpu.VMEM((state_rows, LANES), F32),
            pltpu.VMEM((state_rows, LANES), F32),
            pltpu.SemaphoreType.DMA((chunks,)),
        ],
        compiler_params=params,
        name="second_iteration",
    )(
        cols4, order, order4, follows, last4, inverse4, prob, node_of_scen, root_blocks, node_blocks,
        tiles, cost_r, wide, demand_n, primal2, dual2, sums2, root_mean, node_mean, root_row, node_blocks,
    )
    root_mean, node_mean = comm(root_part, node_part, root_count, width)
    multiplier = pl.pallas_call(
        last_kernel,
        out_shape=shape((state_rows, LANES), F32),
        in_specs=[sm] + [vm] * 5,
        out_specs=vm,
        scratch_shapes=[
            pltpu.VMEM((state_rows, LANES), F32),
            pltpu.VMEM((state_rows, LANES), F32),
        ],
        compiler_params=params,
        name="multiplier_update",
    )(node_of_scen, rest, root_mean, node_mean, root_row, node_blocks)
    return from_rows(primal), from_rows(dual), from_rows(multiplier)


def solution(mesh):
    split = P(("sub", "leaf"), None)
    return jax.shard_map(
        per_device,
        mesh=mesh,
        in_specs=(
            P(), P(), P(), split, split, P(), P(("sub", "leaf")), P(("sub", "leaf")), P(), P(),
        ),
        out_specs=(split, split, split),
        check_vma=False,
    )
```

time: 594 us -> 124 us (0.21); the launches traced: 582 us -> 124 us
  waiting for transfers between devices: 256 us -> 0 us
  matrix products: 152 us -> 0 us
  Pallas kernels: 0 us -> 115 us
  blocking collectives: 82.6 us -> 0 us
  other arithmetic: 45.1 us -> 8.06 us
  local copies, waits for them, and re-layouts: 30.6 us -> 0.01 us
  between operations: 14.6 us -> 0.67 us
    psum x4 -> x0, waiting for transfers between devices: 256 us -> none  [the longest x2 146 us: per_device(): root_mean = lax.psum(root_part, ('sub', 'leaf')) / total_weight]
    dot_general x39 -> x0, matrix products: 152 us -> none  [the longest x4 49.2 us: apply_matrix(): jnp.einsum('snk,nrk->nsr', blocks, tiles, preferred_element_type=jnp.floa...]
    pallas_call x0 -> x5, Pallas kernels: none -> 115 us  [the longest x2 53.7 us: comm(): pl.pallas_call(functools.partial(comm_kernel, ny, nx, nz), out_shape=[jax...]
    psum x2 -> x0, blocking collectives: 82.6 us -> none  [the longest x1 69.8 us: per_device(): total_weight = lax.psum(jnp.sum(prob), ('sub', 'leaf'))]
    unnamed x7 -> x0, other arithmetic: 34.9 us -> none
    transpose x8 -> x0, local copies, waits for them, and re-layouts: 18.8 us -> none  [the longest x4 9.62 us: apply_transpose(): jnp.einsum('nv,nsk->svk', col_select, terms, precision=lax.Precision.HIGH...]
    convert_element_type x8 -> x0, local copies, waits for them, and re-layouts: 11.5 us -> none  [select_blocks(): return picked.astype(jnp.bfloat16)]
  transfers between devices with their start and end apart: 4 -> 0, of which waited for: 4 -> 0; matrix products, arithmetic and copies ran while one was open for 12% -> 0% of each run, Pallas kernels for 0% -> 0%
where the time goes in v1:
time: 124 us
  Pallas kernels  115 us (93%)
  other arithmetic  8.06 us (6%)
    pallas_call x2, Pallas kernels, comm(): pl.pallas_call(functools.partial(comm_kernel, ny, nx, nz), out_shape=[jax...  53.7 us
    pallas_call x1, Pallas kernels, per_device(): pl.pallas_call(functools.partial(second_kernel, chunks, most), out_shape=...  28.4 us
    pallas_call x1, Pallas kernels, per_device(): pl.pallas_call(functools.partial(first_kernel, chunks, most), out_shape=[...  28 us
    pallas_call x1, Pallas kernels, per_device(): pl.pallas_call(last_kernel, out_shape=shape((state_rows, LANES), F32), in...  5.06 us

profile of v1, /device:TPU:1, one launch (start us, length us, event | category | flops | bytes accessed | tf_op | source)
XLA Modules:
  0.0 123.9 jit_solution(8971939803334113428)
XLA Ops:
  0.6 0.9 select_reduce_fusion
  1.5 1.1 convert_reduce_fusion.2
  2.6 1.1 select_reduce_fusion.1
  3.6 0.0 copy-start
  3.6 0.1 slice_compare_fusion
  3.7 0.6 add_convert_fusion.follows
  4.4 1.3 %broadcast_multiply_fusion.1 = (s32[512]{0:T(512)}, s32[512]{0:T(512)}) fusion(s32[512]{0:T(512)S(1)} %select_reduce_fusion, s32[512]{0:T(512)} %param.12), kind=kLoop, calls=%fused_computation.17 | loop fusion | flops 1024 | bytes 8192 | tf_op jit(solution)/shard_map/tables/mul | solution.py:539
  5.6 1.3 %broadcast_multiply_fusion = (s32[512]{0:T(512)}, s32[512]{0:T(512)}) fusion(s32[512]{0:T(512)} %param.11, s32[512]{0:T(512)S(1)} %get-tuple-element.38.order), kind=kLoop, calls=%fused_computation.16 | loop fusion | flops 1024 | bytes 8192 | tf_op jit(solution)/shard_map/tables/mul | solution.py:542
  6.9 1.2 convert_reduce_fusion.1
  8.1 0.6 select_multiply_fusion.last4
  8.7 0.0 copy-done
  8.7 28.0 %first_iteration.1 = (f32[4096,128]{1,0:T(8,128)}, f32[2072,128]{1,0:T(8,128)}, f32[2072,128]{1,0:T(8,128)}, f32[2048,128]{1,0:T(8,128)}, f32[4096,128]{1,0:T(8,...) custom-call(s32[512]{0:T(512)} %get-tuple-element.42.cols4, s32[512]{0:T(512)} %get-tuple-element.39.rows4, s32[512]{0:T(512)} %copy-done, ...), custom_call_target="tpu_custom_call" | custom-call | tf_op jit(solution)/shard_map/first_iteration/pallas_call | solution.py:554
  36.7 29.5 %mean_exchange.2 = (f32[512,128]{1,0:T(8,128)}, f32[1024,128]{1,0:T(8,128)}) custom-call(f32[768,128]{1,0:T(8,128)} %get-tuple-element.24.root_part, f32[1088,128]{1,0:T(8,128)} %get-tuple-element.25.node_part), custom_call_target="tpu_custom_call" | custom-call | tf_op jit(solution)/shard_map/mean_exchange/pallas_call | solution.py:475
  66.1 28.4 %second_iteration.1 = (f32[4096,128]{1,0:T(8,128)}, f32[2048,128]{1,0:T(8,128)}, f32[4096,128]{1,0:T(8,128)}, f32[768,128]{1,0:T(8,128)}, f32[1088,128]{1,0:T(8,128)}) custom-call(s32[512]{0:T(512)} %get-tuple-element.42.cols4, s32[512]{0:T(512)} %copy-done, s32[512]{0:T(512)} %get-tuple-element.40.order4, f32[512]{0:T(512)} %add_convert_fusion.follows, ...), custom_call_target="tpu_custom_call" | custom-call | tf_op jit(solution)/shard_map/second_iteration/pallas_call | solution.py:582
  94.5 24.3 %mean_exchange.3 = (f32[512,128]{1,0:T(8,128)}, f32[1024,128]{1,0:T(8,128)}) custom-call(f32[768,128]{1,0:T(8,128)} %get-tuple-element.31.root_part, f32[1088,128]{1,0:T(8,128)} %get-tuple-element.32.node_part), custom_call_target="tpu_custom_call" | custom-call | tf_op jit(solution)/shard_map/mean_exchange/pallas_call | solution.py:475
  118.8 5.1 %multiplier_update.1 = f32[4096,128]{1,0:T(8,128)} custom-call(s32[4]{0:T(128)} %node_of.5, f32[4096,128]{1,0:T(8,128)} %get-tuple-element.30.rest, f32[512,128]{1,0:T(8,128)} %get-tuple-element.33.root_mean, f32[1024,128]{1,0:T(8,128)} %get-tuple-element.34.node_mean, s32[1,512]{1,0:T(1,128)} %bitcast.33, s32[128,128]{1,0:T(8,128)} %node_row.3), custom_call_target="tpu_custom_call" | custom-call | tf_op jit(solution)/shard_map/multiplier_update/pallas_call | solution.py:612
Async XLA Ops:
  3.6 5.1 %copy-start = (s32[512]{0:T(512)}, s32[512]{0:T(512)S(1)}, u32[]{:S(2)}) copy-start(s32[512]{0:T(512)S(1)} %get-tuple-element.38.order) | copy-start | bytes 6148

commit v2 on v0

v2 whole, which is shorter than its diff:
```python
import functools

import jax
import jax.numpy as jnp
from jax import lax
from jax.experimental import pallas as pl
from jax.experimental.pallas import tpu as pltpu
from jax.sharding import PartitionSpec as P

F32 = jnp.float32
BF16 = jnp.bfloat16
MESH = pl.DeviceIdType.MESH
LANES = 128
PAD = 8


def aligned(value, step=8):
    return pl.multiple_of(value, step)


def top_rows():
    return lax.broadcasted_iota(jnp.int32, (8, LANES), 0) < 4


def unroll_of(count, most):
    step = min(count, most)
    while count % step:
        step -= 1
    return step


def loop(count, most, body, carry=0, first=0):
    step = unroll_of(count, most)

    def outer(i, state):
        base = first + i * step
        return lax.fori_loop(0, step, lambda u, inner: body(base + u, inner), state, unroll=True)

    return lax.fori_loop(0, count // step, outer, carry)


def start_tiles(tiles_hbm, tiles, sems, chunks):
    size = tiles.shape[0] // chunks
    for c in range(chunks):
        part = pl.ds(c * size, size)
        pltpu.make_async_copy(tiles_hbm.at[part], tiles.at[part], sems.at[c]).start()


def wait_tiles(tiles_hbm, tiles, sems, chunks, c):
    size = tiles.shape[0] // chunks
    part = pl.ds(c * size, size)
    pltpu.make_async_copy(tiles_hbm.at[part], tiles.at[part], sems.at[c]).wait()


def pick_pair(ref, first4, second4):
    low = ref[pl.ds(first4 + PAD, 8), :]
    high = ref[pl.ds(second4 + (PAD - 4), 8), :]
    return jnp.where(top_rows(), low, high)


def spread_upper(upper, wide):
    blocks = upper.shape[0]
    for s in range(4):
        wide[pl.ds(s, blocks, stride=4), :] = upper[...]


def pairs_a(tiles, cols4, field, pairs, emit, most):
    def body(p, state):
        lhs = pick_pair(field, cols4[2 * p], cols4[2 * p + 1]).astype(BF16)
        rhs = tiles[pl.ds(2 * p, 2)].reshape(2 * LANES, LANES)
        both = lax.dot_general(lhs, rhs, (((1,), (1,)), ((), ())), preferred_element_type=F32)
        emit(p, jnp.where(top_rows(), both[:, :LANES], both[:, LANES:]))
        return state

    first, count = pairs
    loop(count, most, body, 0, first)


def transpose_pass(tiles, order, order4, follows, dual, sums, pairs, carry, most):
    def body(p, carry):
        a, b = 2 * p, 2 * p + 1
        top = top_rows()
        low = dual[pl.ds(order4[a] + PAD, 8), :]
        high = dual[pl.ds(order4[b] + (PAD - 4), 8), :]
        lhs = jnp.concatenate([jnp.where(top, low, 0.0), jnp.where(top, 0.0, high)], axis=1)
        rhs = jnp.concatenate([tiles[order[a]], tiles[order[b]]], axis=0)
        own = lax.dot_general(
            lhs.astype(BF16), rhs, (((1,), (0,)), ((), ())), preferred_element_type=F32
        )
        fa, fb = follows[a], follows[b]
        other = pltpu.roll(own, 4, 0)
        within = own + jnp.where(top, 0.0, fb) * other
        full = jnp.where(top, fb * own + other, within)
        both = fa * fb
        sums[pl.ds(aligned(PAD + 8 * p), 8), :] = within + jnp.where(top, fa, both) * carry
        return both * carry + full

    first, count = pairs
    return loop(count, most, body, carry, first)


def first_step(cost, wide, field):
    rows = cost.shape[0]

    def body(i, state):
        at = aligned(16 * i, 16)
        moved = -cost[pl.ds(at, 16), :].astype(F32) * 0.5
        field[pl.ds(at + PAD, 16), :] = 2.0 * jnp.clip(moved, 0.0, wide[pl.ds(at, 16), :])
        return state

    loop(rows // 16, 8, body)


def later_step(cost, wide, sums, last4, base, primal_out, field, old):
    rows = cost.shape[0]

    def body(i, state):
        at = aligned(16 * i, 16)
        gradient = jnp.concatenate(
            [
                pick_pair(sums, last4[4 * i], last4[4 * i + 1]),
                pick_pair(sums, last4[4 * i + 2], last4[4 * i + 3]),
            ],
            axis=0,
        )
        before = old(at)
        moved = base(at, before) - cost[pl.ds(at, 16), :].astype(F32) + gradient
        after = jnp.clip(moved * 0.5, 0.0, wide[pl.ds(at, 16), :])
        primal_out[pl.ds(at, 16), :] = after
        field[pl.ds(at + PAD, 16), :] = 2.0 * after - before
        return state

    loop(rows // 16, 8, body)


def weigh_root(primal, prob, root_blocks, total, root_part):
    blocks = total.shape[0]
    acc = prob[0] * primal[pl.ds(0, blocks, stride=4), :]
    for s in range(1, 4):
        acc = acc + prob[s] * primal[pl.ds(s, blocks, stride=4), :]
    total[...] = acc
    root_count = root_blocks.shape[0]
    pieces = (root_part.shape[0] - root_count) // 8
    each = root_count // pieces
    split = each + 8
    weight = jnp.full((8, LANES), prob[0] + prob[1] + prob[2] + prob[3], F32)

    def body(i, state):
        for u in range(each):
            root_part[pl.ds(i * split + u, 1), :] = total[pl.ds(root_blocks[i * each + u], 1), :]
        root_part[pl.ds(aligned(i * split + each), 8), :] = weight
        return state

    lax.fori_loop(0, pieces, body, 0)


def weigh_nodes(primal, prob, node_of, local_of, node_blocks, vals, node_part):
    width = node_part.shape[0] // 8 - 8
    for s in range(4):
        base = node_of[s] * width

        def body(b, state):
            row = primal[pl.ds(4 * node_blocks[base + b] + s, 1), :]
            vals[pl.ds(s * width + b, 1), :] = row
            return state

        loop(width, 16, body)
    for m in range(8):
        slot = m
        share = []
        for s in range(4):
            gap = local_of[s] - m
            share.append(prob[s] * (1 - jnp.minimum(gap * gap, 1)).astype(F32))
        part = share[0] * vals[pl.ds(0, width), :]
        for s in range(1, 4):
            part = part + share[s] * vals[pl.ds(s * width, width), :]
        node_part[pl.ds(slot * (width + 8), width), :] = part
        node_part[pl.ds(slot * (width + 8) + width, 8), :] = jnp.full(
            (8, LANES), share[0] + share[1] + share[2] + share[3], F32
        )


def split_two(value):
    high = value.astype(BF16)
    low = (value - high.astype(F32)).astype(BF16)
    return jnp.concatenate([high, low], axis=1)


def mark_blocks(root_row, node_row, node_of, hot_root, hot_node, mask):
    blocks = hot_root.shape[0]
    chunk = min(blocks, 128)
    width = hot_node.shape[1]
    count = hot_root.shape[1]
    ones_root = jnp.ones((count, LANES), BF16)
    ones_node = jnp.ones((width, LANES), BF16)

    def body(i, state):
        at = aligned(i * chunk, chunk)
        here = lax.broadcasted_iota(jnp.int32, (chunk, count), 0) + at
        hot = (here == root_row[...]).astype(F32).astype(BF16)
        hot_root[pl.ds(at, chunk), :] = hot
        root_mask = jnp.dot(hot, ones_root, preferred_element_type=F32)
        here = lax.broadcasted_iota(jnp.int32, (chunk, width), 0) + at
        for s in range(4):
            hot = (here == node_row[pl.ds(node_of[s], 1), :]).astype(F32).astype(BF16)
            hot_node[pl.ds(aligned(s * blocks + at, chunk), chunk), :] = hot
            mask[pl.ds(4 * at + s, chunk, stride=4), :] = root_mask + jnp.dot(
                hot, ones_node, preferred_element_type=F32
            )
        return state

    lax.fori_loop(0, blocks // chunk, body, 0)


def fill_means(root_mean, node_mean, hot_root, hot_node, local_of, filled):
    blocks = hot_root.shape[0]
    chunk = min(blocks, 128)
    width = node_mean.shape[0] // 8
    root_rhs = split_two(root_mean[...])
    node_rhs = []
    for s in range(4):
        start = local_of[s] * width
        node_rhs.append(split_two(node_mean[pl.ds(start, width), :]))

    def body(i, state):
        at = aligned(i * chunk, chunk)
        got = jnp.dot(hot_root[pl.ds(at, chunk), :], root_rhs, preferred_element_type=F32)
        root_fill = got[:, :LANES] + got[:, LANES:]
        for s in range(4):
            hot = hot_node[pl.ds(aligned(s * blocks + at, chunk), chunk), :]
            got = jnp.dot(hot, node_rhs[s], preferred_element_type=F32)
            filled[pl.ds(4 * at + s, chunk, stride=4), :] = (
                root_fill + got[:, :LANES] + got[:, LANES:]
            )
        return state

    lax.fori_loop(0, blocks // chunk, body, 0)


def wait_bytes(ref, sem):
    pltpu.make_async_copy(ref, ref, sem).wait()


class Exchange:
    def __init__(self, ny, nx, nz, bufs, send, recv):
        (self.root_part, self.node_part, self.r0, self.n0, self.rsum, self.nsum, self.r1, self.n1,
         self.rz, self.r2, self.root_all, self.node_all) = bufs
        self.send, self.recv = send, recv
        sub, leaf = lax.axis_index("sub"), lax.axis_index("leaf")
        z, core = sub // 2, sub % 2
        y, x = leaf // nx, leaf % nx
        self.z, self.core, self.leaf, self.nz = z, core, leaf, nz
        self.cells = ny * nx
        self.chunk = self.rsum.shape[0] // self.cells
        self.rows = self.nsum.shape[0] // nz
        self.partner = {"sub": z * 2 + (1 - core), "leaf": leaf}
        self.plane, self.column = [], []
        for k in range(1, self.cells):
            other = ((y + k // nx) % ny) * nx + (x + k % nx) % nx
            self.plane.append((k, other, {"sub": sub, "leaf": other}))
        for k in range(1, nz):
            other = (z + k) % nz
            self.column.append((k, other, {"sub": other * 2 + core, "leaf": leaf}))
        self.peers = [self.partner] + [p[2] for p in self.plane] + [p[2] for p in self.column]

    def push(self, src, dst, which, peer):
        pltpu.make_async_remote_copy(
            src_ref=src, dst_ref=dst, send_sem=self.send.at[which], recv_sem=self.recv.at[which],
            device_id=peer, device_id_type=MESH,
        ).start()

    def root_to_partner(self):
        half = self.cells * self.chunk
        src = self.root_part.at[pl.ds(aligned((1 - self.core) * half), half)]
        self.push(src, self.r0, 1, self.partner)

    def node_to_partner(self):
        half = self.nz * self.rows
        src = self.node_part.at[pl.ds(aligned((1 - self.core) * half), half)]
        self.push(src, self.n0, 0, self.partner)

    def root_to_plane(self):
        half = self.cells * self.chunk
        wait_bytes(self.r0, self.recv.at[1])
        self.rsum[...] = self.root_part[pl.ds(aligned(self.core * half), half), :] + self.r0[...]
        for k, other, peer in self.plane:
            self.push(
                self.rsum.at[pl.ds(aligned(other * self.chunk), self.chunk)],
                self.r1.at[pl.ds((k - 1) * self.chunk, self.chunk)], 3, peer,
            )

    def node_to_column(self):
        half = self.nz * self.rows
        wait_bytes(self.n0, self.recv.at[0])
        self.nsum[...] = self.node_part[pl.ds(aligned(self.core * half), half), :] + self.n0[...]
        for k, other, peer in self.column:
            self.push(
                self.nsum.at[pl.ds(aligned(other * self.rows), self.rows)],
                self.n1.at[pl.ds((k - 1) * self.rows, self.rows)], 2, peer,
            )

    def node_back(self):
        width = self.rows - 8
        wait_bytes(self.n1, self.recv.at[2])
        acc = self.nsum[pl.ds(aligned(self.z * self.rows), self.rows), :]
        for k in range(1, self.nz):
            acc = acc + self.n1[pl.ds((k - 1) * self.rows, self.rows), :]
        spot = pl.ds(aligned((self.core * self.nz + self.z) * width), width)
        self.node_all[spot, :] = acc[:width] / acc[width:width + 1]
        for k, other, peer in self.column:
            self.push(self.node_all.at[spot], self.node_all.at[spot], 4, peer)

    def root_to_column(self):
        wait_bytes(self.r1, self.recv.at[3])
        acc = self.rsum[pl.ds(aligned(self.leaf * self.chunk), self.chunk), :]
        for k in range(1, self.cells):
            acc = acc + self.r1[pl.ds((k - 1) * self.chunk, self.chunk), :]
        self.rz[...] = acc
        for k, other, peer in self.column:
            self.push(self.rz, self.r2.at[pl.ds((k - 1) * self.chunk, self.chunk)], 5, peer)

    def root_back(self):
        keep = self.chunk - 8
        wait_bytes(self.r2, self.recv.at[5])
        total = self.rz[...]
        for k in range(1, self.nz):
            total = total + self.r2[pl.ds((k - 1) * self.chunk, self.chunk), :]
        spot = pl.ds(aligned((self.core * self.cells + self.leaf) * keep), keep)
        self.root_all[spot, :] = total[:keep] / total[keep:keep + 1]
        for k, other, peer in self.plane:
            self.push(self.root_all.at[spot], self.root_all.at[spot], 7, peer)

    def node_home(self):
        half = self.nz * (self.rows - 8)
        wait_bytes(self.node_all.at[pl.ds(0, half - (self.rows - 8))], self.recv.at[4])
        spot = self.node_all.at[pl.ds(aligned(self.core * half), half)]
        self.push(spot, spot, 6, self.partner)

    def root_home(self):
        keep = self.chunk - 8
        half = self.cells * keep
        wait_bytes(self.root_all.at[pl.ds(0, half - keep)], self.recv.at[7])
        spot = self.root_all.at[pl.ds(aligned(self.core * half), half)]
        self.push(spot, spot, 8, self.partner)

    def finish(self):
        wait_bytes(self.node_all.at[pl.ds(0, self.nz * (self.rows - 8))], self.recv.at[6])
        wait_bytes(self.root_all.at[pl.ds(0, self.cells * (self.chunk - 8))], self.recv.at[8])

    def drain(self):
        width, keep = self.rows - 8, self.chunk - 8
        sent = [
            self.n0, self.r0, self.n1, self.r1,
            self.node_all.at[pl.ds(0, (self.nz - 1) * width)],
            self.r2,
            self.node_all.at[pl.ds(0, self.nz * width)],
            self.root_all.at[pl.ds(0, (self.cells - 1) * keep)],
            self.root_all.at[pl.ds(0, self.cells * keep)],
        ]
        for which, ref in enumerate(sent):
            wait_bytes(ref, self.send.at[which])


def whole_kernel(
    chunks, most, ny, nx, nz,
    cols4, rows4, order, order4, follows, last4, inverse4, prob, node_of, local_of, root_blocks, node_blocks,
    tiles_hbm, cost, demand, upper, root_row, node_row,
    primal_hbm, dual_hbm, multiplier_hbm,
    tiles, field, wide, demand_f, demand_n, dual, sums, second, third, last, filled, mask, rest,
    dual_rows, total, vals, hot_root, hot_node, *others,
):
    bufs, (sems, out_sems, send0, recv0, send1, recv1) = others[:24], others[24:]
    rounds = [
        Exchange(ny, nx, nz, bufs[:12], send0, recv0),
        Exchange(ny, nx, nz, bufs[12:], send1, recv1),
    ]
    start_tiles(tiles_hbm, tiles, sems, chunks)
    barrier = pltpu.get_barrier_semaphore()
    for peer in rounds[0].peers:
        pl.semaphore_signal(barrier, inc=1, device_id=peer, device_id_type=MESH)
    pairs = tiles.shape[0] // 2
    per_chunk = pairs // chunks
    rows = cost.shape[0]
    zero = jnp.zeros((8, LANES), F32)
    sums[pl.ds(PAD + 8 * pairs, 8), :] = zero

    spread_upper(upper, wide)
    demand_f[pl.ds(PAD, demand.shape[0]), :] = demand[...].astype(F32)
    first_step(cost, wide, field)

    def emit_first(p, image):
        want = pick_pair(demand_f, rows4[2 * p], rows4[2 * p + 1])
        demand_n[pl.ds(aligned(8 * p), 8), :] = want
        dual[pl.ds(aligned(PAD + 8 * p), 8), :] = jnp.maximum(0.25 * (want - image), 0.0)

    def emit_next(p, image):
        at = aligned(8 * p)
        old = dual[pl.ds(aligned(at + PAD), 8), :]
        dual[pl.ds(aligned(at + PAD), 8), :] = jnp.maximum(
            old + 0.25 * (demand_n[pl.ds(at, 8), :] - image), 0.0
        )

    def chunk_body(c, state):
        wait_tiles(tiles_hbm, tiles, sems, chunks, c)
        pairs_a(tiles, cols4, field, (c * per_chunk, per_chunk), emit_first, most)
        return state

    def forward(part):
        first, stop = part[0] * pairs // 8, part[1] * pairs // 8
        pairs_a(tiles, cols4, field, (first, stop - first), emit_next, most)

    def backward(part, carry):
        first, stop = part[0] * pairs // 8, part[1] * pairs // 8
        return transpose_pass(
            tiles, order, order4, follows, dual, sums, (first, stop - first), carry, most
        )

    lax.fori_loop(0, chunks, chunk_body, 0)
    backward((0, 8), zero)
    later_step(
        cost, wide, sums, last4, lambda at, before: before, second, field,
        lambda at: 0.5 * field[pl.ds(at + PAD, 16), :],
    )

    go = rounds[0]
    weigh_root(second, prob, root_blocks, total, go.root_part)
    pl.semaphore_wait(barrier, len(go.peers))
    go.root_to_partner()
    weigh_nodes(second, prob, node_of, local_of, node_blocks, vals, go.node_part)
    go.node_to_partner()
    go.root_to_plane()
    forward((0, 2))
    go.node_to_column()
    forward((2, 8))
    go.root_to_column()
    carry = backward((0, 2), zero)
    go.node_back()
    carry = backward((2, 6), carry)
    go.root_back()
    carry = backward((6, 8), carry)
    mark_blocks(root_row, node_row, node_of, hot_root, hot_node, mask)
    go.node_home()
    go.root_home()
    go.finish()
    fill_means(go.root_all, go.node_all, hot_root, hot_node, local_of, filled)

    def consensus(at, before):
        return jnp.where(mask[pl.ds(at, 16), :] > 0.5, filled[pl.ds(at, 16), :], before)

    later_step(
        cost, wide, sums, last4, lambda at, before: 2.0 * consensus(at, before), third, field,
        lambda at: second[pl.ds(at, 16), :],
    )
    forward((0, 8))
    backward((0, 8), zero)

    def pull(at, before):
        start = second[pl.ds(at, 16), :]
        middle = consensus(at, start)
        return before - (start - middle) + middle

    later_step(
        cost, wide, sums, last4, pull, last, field, lambda at: third[pl.ds(at, 16), :],
    )
    primal_copy = pltpu.make_async_copy(last, primal_hbm, out_sems.at[0])
    primal_copy.start()

    go = rounds[1]
    weigh_root(last, prob, root_blocks, total, go.root_part)
    go.root_to_partner()
    weigh_nodes(last, prob, node_of, local_of, node_blocks, vals, go.node_part)
    go.node_to_partner()
    go.root_to_plane()
    forward((0, 2))
    go.node_to_column()
    forward((2, 8))
    go.root_to_column()

    def order_body(r, state):
        dual_rows[pl.ds(aligned(8 * r), 8), :] = pick_pair(
            dual, inverse4[2 * r], inverse4[2 * r + 1]
        )
        return state

    loop(pairs, 16, order_body)
    dual_copy = pltpu.make_async_copy(dual_rows, dual_hbm, out_sems.at[1])
    dual_copy.start()
    go.node_back()

    def rest_body(i, state):
        at = aligned(16 * i, 16)
        start = second[pl.ds(at, 16), :]
        rest[pl.ds(at, 16), :] = start - consensus(at, start) + last[pl.ds(at, 16), :]
        return state

    loop(rows // 16, 8, rest_body)
    go.root_back()
    go.node_home()
    go.root_home()
    go.finish()
    fill_means(go.root_all, go.node_all, hot_root, hot_node, local_of, filled)

    def final_body(i, state):
        at = aligned(16 * i, 16)
        left = rest[pl.ds(at, 16), :] - filled[pl.ds(at, 16), :]
        third[pl.ds(at, 16), :] = jnp.where(mask[pl.ds(at, 16), :] > 0.5, left, 0.0)
        return state

    loop(rows // 16, 8, final_body)
    multiplier_copy = pltpu.make_async_copy(third, multiplier_hbm, out_sems.at[2])
    multiplier_copy.start()
    primal_copy.wait()
    dual_copy.wait()
    rounds[0].drain()
    rounds[1].drain()
    multiplier_copy.wait()


def as_rows(field):
    count, size = field.shape
    return field.reshape(count, size // LANES, LANES).transpose(1, 0, 2).reshape(-1, LANES)


def from_rows(rows):
    blocks = rows.shape[0] // 4
    return rows.reshape(blocks, 4, LANES).transpose(1, 0, 2).reshape(4, blocks * LANES)


def per_device(
    tiles, tile_rows, tile_cols, cost, demand, upper, prob, node_of_scen, root_blocks, node_blocks
):
    nt = tiles.shape[0]
    nvt = cost.shape[1] // LANES
    nct = demand.shape[1] // LANES
    width = node_blocks.shape[1]
    root_count = root_blocks.shape[0]
    leaf = lax.axis_size("leaf")
    chunks = 8
    most = 32
    with jax.named_scope("tables"):
        n = jnp.arange(nt, dtype=jnp.int32)
        ahead = (tile_cols[None, :] < tile_cols[:, None]) | (
            (tile_cols[None, :] == tile_cols[:, None]) & (n[None, :] < n[:, None])
        )
        rank = jnp.sum(ahead.astype(jnp.int32), axis=1)
        place = rank[None, :] == n[:, None]
        order = jnp.sum(jnp.where(place, n[None, :], 0), axis=1)
        sorted_col = jnp.sum(jnp.where(place, tile_cols[None, :], 0), axis=1)
        follows = jnp.concatenate(
            [jnp.zeros((1,), F32), (sorted_col[1:] == sorted_col[:-1]).astype(F32)]
        )
        v = jnp.arange(nvt, dtype=jnp.int32)
        upto = jnp.sum((tile_cols[None, :] <= v[:, None]).astype(jnp.int32), axis=1)
        has = jnp.sum((tile_cols[None, :] == v[:, None]).astype(jnp.int32), axis=1)
        last4 = 4 * jnp.where(has > 0, upto - 1, nt)
        inverse4 = 4 * jnp.sum(
            jnp.where(tile_rows[None, :] == jnp.arange(nct)[:, None], n[None, :], 0), axis=1
        )
        cols4, rows4, order4 = 4 * tile_cols, 4 * tile_rows, 4 * order
    local_of = node_of_scen - 8 * lax.axis_index("leaf")
    cost_r, demand_r = as_rows(cost), as_rows(demand)
    upper_r = upper.reshape(nvt, LANES)
    root_row = root_blocks.reshape(1, root_count)
    sub = lax.axis_size("sub")
    nz = sub // 2
    ny = 4 if leaf == 16 else 1
    nx = leaf // ny
    chunk = root_count // (2 * leaf) + 8
    node_rows = width + 8
    pad_rows = PAD + 4 * nt + 16
    state_rows = 4 * nvt
    sm = pl.BlockSpec(memory_space=pltpu.SMEM)
    vm = pl.BlockSpec(memory_space=pltpu.VMEM)
    hbm = pl.BlockSpec(memory_space=pl.ANY)

    def lines(count):
        return pltpu.VMEM((count, LANES), F32)

    exchange = [
        lines(2 * leaf * chunk),
        lines(8 * node_rows),
        lines(leaf * chunk),
        lines(nz * node_rows),
        lines(leaf * chunk),
        lines(nz * node_rows),
        lines((leaf - 1) * chunk),
        lines((nz - 1) * node_rows),
        lines(chunk),
        lines((nz - 1) * chunk),
        lines(root_count),
        lines(8 * width),
    ]
    primal, dual, multiplier = pl.pallas_call(
        functools.partial(whole_kernel, chunks, most, ny, nx, nz),
        out_shape=[
            jax.ShapeDtypeStruct((state_rows, LANES), F32),
            jax.ShapeDtypeStruct((4 * nct, LANES), F32),
            jax.ShapeDtypeStruct((state_rows, LANES), F32),
        ],
        in_specs=[sm] * 12 + [hbm] + [vm] * 5,
        out_specs=[hbm] * 3,
        scratch_shapes=[
            pltpu.VMEM(tiles.shape, BF16),
            lines(state_rows + 2 * PAD),
            lines(state_rows),
            lines(4 * nct + 2 * PAD),
            lines(4 * nt),
            lines(pad_rows),
            lines(pad_rows),
            lines(state_rows),
            lines(state_rows),
            lines(state_rows),
            lines(state_rows),
            lines(state_rows),
            lines(state_rows),
            lines(4 * nct),
            lines(nvt),
            lines(4 * width),
            pltpu.VMEM((nvt, root_count), BF16),
            pltpu.VMEM((4 * nvt, width), BF16),
            *exchange,
            *exchange,
            pltpu.SemaphoreType.DMA((chunks,)),
            pltpu.SemaphoreType.DMA((3,)),
            *[pltpu.SemaphoreType.DMA((9,))] * 4,
        ],
        compiler_params=pltpu.CompilerParams(
            collective_id=0, has_side_effects=True, vmem_limit_bytes=62 * 1024 * 1024
        ),
        name="hedging",
    )(
        cols4, rows4, order, order4, follows, last4, inverse4, prob, node_of_scen, local_of,
        root_blocks, node_blocks.reshape(-1), tiles, cost_r, demand_r, upper_r, root_row, node_blocks,
    )
    return from_rows(primal), from_rows(dual), from_rows(multiplier)


def solution(mesh):
    split = P(("sub", "leaf"), None)
    return jax.shard_map(
        per_device,
        mesh=mesh,
        in_specs=(
            P(), P(), P(), split, split, P(), P(("sub", "leaf")), P(("sub", "leaf")), P(), P(),
        ),
        out_specs=(split, split, split),
        check_vma=False,
    )
```

time: 594 us -> 88.8 us (0.15); the launches traced: 582 us -> 88.5 us
  waiting for transfers between devices: 256 us -> 0 us
  matrix products: 152 us -> 0 us
  blocking collectives: 82.6 us -> 0 us
  Pallas kernels: 0 us -> 72.8 us
  other arithmetic: 45.1 us -> 8.64 us
  local copies, waits for them, and re-layouts: 30.6 us -> 6.43 us
  between operations: 14.6 us -> 0.67 us
    psum x4 -> x0, waiting for transfers between devices: 256 us -> none  [the longest x2 146 us: per_device(): root_mean = lax.psum(root_part, ('sub', 'leaf')) / total_weight]
    dot_general x39 -> x0, matrix products: 152 us -> none  [the longest x4 49.2 us: apply_matrix(): jnp.einsum('snk,nrk->nsr', blocks, tiles, preferred_element_type=jnp.floa...]
    psum x2 -> x0, blocking collectives: 82.6 us -> none  [the longest x1 69.8 us: per_device(): total_weight = lax.psum(jnp.sum(prob), ('sub', 'leaf'))]
    pallas_call x0 -> x1, Pallas kernels: none -> 72.8 us  [per_device(): pl.pallas_call(functools.partial(whole_kernel, chunks, most, ny, nx, nz),...]
    unnamed x7 -> x0, other arithmetic: 34.9 us -> none
    transpose x8 -> x0, local copies, waits for them, and re-layouts: 18.8 us -> none  [the longest x4 9.62 us: apply_transpose(): jnp.einsum('nv,nsk->svk', col_select, terms, precision=lax.Precision.HIGH...]
    convert_element_type x8 -> x0, local copies, waits for them, and re-layouts: 11.5 us -> none  [select_blocks(): return picked.astype(jnp.bfloat16)]
    unnamed x36 -> x9, local copies, waits for them, and re-layouts: 0.35 us -> 6.43 us
  transfers between devices with their start and end apart: 4 -> 0, of which waited for: 4 -> 0; matrix products, arithmetic and copies ran while one was open for 12% -> 0% of each run, Pallas kernels for 0% -> 0%
where the time goes in v2:
time: 88.8 us; the launch traced here: 88.5 us
  Pallas kernels  72.8 us (82%)
  other arithmetic  8.64 us (10%)
  local copies, waits for them, and re-layouts  6.43 us (7%)
    pallas_call x1, Pallas kernels, per_device(): pl.pallas_call(functools.partial(whole_kernel, chunks, most, ny, nx, nz),...  72.8 us
    unnamed x9, local copies, waits for them, and re-layouts  6.43 us

profile of v2, /device:TPU:1, one launch (start us, length us, event | category | flops | bytes accessed | tf_op | source)
XLA Modules:
  0.0 88.5 jit_solution(9399350295220044679)
XLA Ops:
  0.6 1.2 %broadcast_subtract_fusion.local_of = s32[4]{0:T(128)} fusion(s32[4]{0:T(128)} %node_of.1, s32[]{:T(128)S(6)} %mul_shard_map.3), kind=kLoop, calls=%fused_computation.20 | loop fusion | flops 4 | bytes 36 | tf_op jit(solution)/shard_map/sub | solution.py:560
  1.8 0.9 select_reduce_fusion
  2.7 1.1 %convert_reduce_fusion.2 = s32[512]{0:T(512)S(1)} fusion(s32[512]{0:T(512)} %param.12), kind=kLoop, calls=%fused_computation.9 | loop fusion | flops 1834496 | bytes 4096 | tf_op jit(solution)/shard_map/tables/reduce_sum | solution.py:545
  3.8 1.1 %select_reduce_fusion.1 = (s32[512]{0:T(512)S(1)}, s32[512]{0:T(512)S(1)}) fusion(s32[512]{0:T(512)S(1)} %convert_reduce_fusion.2, s32[512]{0:T(512)} %param.12), kind=kLoop, calls=%fused_computation.6 | loop fusion | flops 1309696 | bytes 8192 | tf_op jit(solution)/shard_map/tables/reduce_sum | solution.py:548
  4.8 0.0 copy-start.2
  4.8 0.1 slice_compare_fusion
  4.9 0.7 add_convert_fusion.follows
  5.6 0.6 broadcast_multiply_fusion
  6.2 1.3 %broadcast_multiply_fusion.2 = (s32[512]{0:T(512)}, s32[512]{0:T(512)}) fusion(s32[512]{0:T(512)} %param.11, s32[512]{0:T(512)} %param.12), kind=kLoop, calls=%fused_computation.18 | loop fusion | flops 1024 | bytes 8192 | tf_op jit(solution)/shard_map/tables/mul | solution.py:559
  7.5 1.2 %convert_reduce_fusion.1 = (s32[1024]{0:T(1024)S(1)}, s32[1024]{0:T(1024)S(1)}) fusion(s32[512]{0:T(512)} %param.12), kind=kLoop, calls=%fused_computation.2 | loop fusion | flops 3143680 | bytes 10240 | tf_op jit(solution)/shard_map/tables/reduce_sum | solution.py:554
  8.7 0.6 select_multiply_fusion.last4
  9.3 0.0 copy-done.2
  9.3 72.8 %hedging.1 = (f32[4096,128]{1,0:T(8,128)}, f32[2048,128]{1,0:T(8,128)}, f32[4096,128]{1,0:T(8,128)}) custom-call(s32[512]{0:T(512)} %get-tuple-element.16.cols4, s32[512]{0:T(512)} %get-tuple-element.15.rows4, s32[512]{0:T(512)} %copy-done.2, s32[512]{0:T(512)} %get-tuple-element.14.order4, f32[512]{0:T(512)} %add_convert_fusion.follows, ...), custom_call_target="tpu_custom_call" | custom-call | tf_op jit(solution)/shard_map/hedging/pallas_call | solution.py:593
  82.1 0.0 copy-start.1
  82.1 3.1 %copy.26 = f32[4,131072]{1,0:T(4,128)} copy(f32[4,131072]{1,0:T(4,128)} %bitcast.29) | data formatting | bytes 4194304
  85.2 0.0 copy-done.1
  85.2 0.0 copy-start
  85.2 1.0 %copy.27 = f32[4,65536]{1,0:T(4,128)} copy(f32[4,65536]{1,0:T(4,128)S(1)} %bitcast.30) | data formatting | bytes 2097152
  86.2 1.0 %copy-done = f32[4096,128]{1,0:T(8,128)S(1)} copy-done((f32[4096,128]{1,0:T(8,128)S(1)}, f32[4096,128]{1,0:T(8,128)}, u32[]{:S(2)}) %copy-start) | copy-done | bytes 2097176
  87.2 1.3 %copy.28 = f32[4,131072]{1,0:T(4,128)} copy(f32[4,131072]{1,0:T(4,128)S(1)} %bitcast.28) | data formatting | bytes 4194304
Async XLA Ops:
  4.8 4.5 %copy-start.2 = (s32[512]{0:T(512)}, s32[512]{0:T(512)S(1)}, u32[]{:S(2)}) copy-start(s32[512]{0:T(512)S(1)} %get-tuple-element.12.order) | copy-start | bytes 6148
  82.1 3.1 %copy-start.1 = (f32[2048,128]{1,0:T(8,128)S(1)}, f32[2048,128]{1,0:T(8,128)}, u32[]{:S(2)}) copy-start(f32[2048,128]{1,0:T(8,128)} %get-tuple-element.7) | copy-start | bytes 3145732
  85.2 2.0 %copy-start = (f32[4096,128]{1,0:T(8,128)S(1)}, f32[4096,128]{1,0:T(8,128)}, u32[]{:S(2)}) copy-start(f32[4096,128]{1,0:T(8,128)} %get-tuple-element.8) | copy-start | bytes 6291460

commit v3 on v2

--- a/solution.py
+++ b/solution.py
@@ -212,9 +212,9 @@
     lax.fori_loop(0, blocks // chunk, body, 0)
 
 
-def fill_means(root_mean, node_mean, hot_root, hot_node, local_of, filled):
+def fill_means(root_mean, node_mean, hot_root, hot_node, local_of, emit):
     blocks = hot_root.shape[0]
-    chunk = min(blocks, 128)
+    chunk = min(blocks, 256)
     width = node_mean.shape[0] // 8
     root_rhs = split_two(root_mean[...])
     node_rhs = []
@@ -229,8 +229,8 @@
         for s in range(4):
             hot = hot_node[pl.ds(aligned(s * blocks + at, chunk), chunk), :]
             got = jnp.dot(hot, node_rhs[s], preferred_element_type=F32)
-            filled[pl.ds(4 * at + s, chunk, stride=4), :] = (
-                root_fill + got[:, :LANES] + got[:, LANES:]
+            emit(
+                pl.ds(4 * at + s, chunk, stride=4), root_fill + got[:, :LANES] + got[:, LANES:]
             )
         return state
 
@@ -365,11 +365,11 @@
     chunks, most, ny, nx, nz,
     cols4, rows4, order, order4, follows, last4, inverse4, prob, node_of, local_of, root_blocks, node_blocks,
     tiles_hbm, cost, demand, upper, root_row, node_row,
-    primal_hbm, dual_hbm, multiplier_hbm,
-    tiles, field, wide, demand_f, demand_n, dual, sums, second, third, last, filled, mask, rest,
-    dual_rows, total, vals, hot_root, hot_node, *others,
+    last, dual_rows, multiplier,
+    tiles, field, wide, demand_f, demand_n, dual, sums, second, third, filled, mask, rest,
+    total, vals, hot_root, hot_node, *others,
 ):
-    bufs, (sems, out_sems, send0, recv0, send1, recv1) = others[:24], others[24:]
+    bufs, (sems, send0, recv0, send1, recv1) = others[:24], others[24:]
     rounds = [
         Exchange(ny, nx, nz, bufs[:12], send0, recv0),
         Exchange(ny, nx, nz, bufs[12:], send1, recv1),
@@ -442,7 +442,11 @@
     go.node_home()
     go.root_home()
     go.finish()
-    fill_means(go.root_all, go.node_all, hot_root, hot_node, local_of, filled)
+
+    def keep_means(at, means):
+        filled[at, :] = means
+
+    fill_means(go.root_all, go.node_all, hot_root, hot_node, local_of, keep_means)
 
     def consensus(at, before):
         return jnp.where(mask[pl.ds(at, 16), :] > 0.5, filled[pl.ds(at, 16), :], before)
@@ -462,8 +466,6 @@
     later_step(
         cost, wide, sums, last4, pull, last, field, lambda at: third[pl.ds(at, 16), :],
     )
-    primal_copy = pltpu.make_async_copy(last, primal_hbm, out_sems.at[0])
-    primal_copy.start()
 
     go = rounds[1]
     weigh_root(last, prob, root_blocks, total, go.root_part)
@@ -483,8 +485,6 @@
         return state
 
     loop(pairs, 16, order_body)
-    dual_copy = pltpu.make_async_copy(dual_rows, dual_hbm, out_sems.at[1])
-    dual_copy.start()
     go.node_back()
 
     def rest_body(i, state):
@@ -498,22 +498,13 @@
     go.node_home()
     go.root_home()
     go.finish()
-    fill_means(go.root_all, go.node_all, hot_root, hot_node, local_of, filled)
-
-    def final_body(i, state):
-        at = aligned(16 * i, 16)
-        left = rest[pl.ds(at, 16), :] - filled[pl.ds(at, 16), :]
-        third[pl.ds(at, 16), :] = jnp.where(mask[pl.ds(at, 16), :] > 0.5, left, 0.0)
-        return state
-
-    loop(rows // 16, 8, final_body)
-    multiplier_copy = pltpu.make_async_copy(third, multiplier_hbm, out_sems.at[2])
-    multiplier_copy.start()
-    primal_copy.wait()
-    dual_copy.wait()
+
+    def update(at, means):
+        multiplier[at, :] = jnp.where(mask[at, :] > 0.5, rest[at, :] - means, 0.0)
+
+    fill_means(go.root_all, go.node_all, hot_root, hot_node, local_of, update)
     rounds[0].drain()
     rounds[1].drain()
-    multiplier_copy.wait()
 
 
 def as_rows(field):
@@ -535,8 +526,8 @@
     width = node_blocks.shape[1]
     root_count = root_blocks.shape[0]
     leaf = lax.axis_size("leaf")
-    chunks = 8
-    most = 32
+    chunks = 4
+    most = 64
     with jax.named_scope("tables"):
         n = jnp.arange(nt, dtype=jnp.int32)
         ahead = (tile_cols[None, :] < tile_cols[:, None]) | (
@@ -592,13 +583,9 @@
     ]
     primal, dual, multiplier = pl.pallas_call(
         functools.partial(whole_kernel, chunks, most, ny, nx, nz),
-        out_shape=[
-            jax.ShapeDtypeStruct((state_rows, LANES), F32),
-            jax.ShapeDtypeStruct((4 * nct, LANES), F32),
-            jax.ShapeDtypeStruct((state_rows, LANES), F32),
-        ],
+        out_shape=[lines(state_rows), lines(4 * nct), lines(state_rows)],
         in_specs=[sm] * 12 + [hbm] + [vm] * 5,
-        out_specs=[hbm] * 3,
+        out_specs=[vm] * 3,
         scratch_shapes=[
             pltpu.VMEM(tiles.shape, BF16),
             lines(state_rows + 2 * PAD),
@@ -612,8 +599,6 @@
             lines(state_rows),
             lines(state_rows),
             lines(state_rows),
-            lines(state_rows),
-            lines(4 * nct),
             lines(nvt),
             lines(4 * width),
             pltpu.VMEM((nvt, root_count), BF16),
@@ -621,11 +606,10 @@
             *exchange,
             *exchange,
             pltpu.SemaphoreType.DMA((chunks,)),
-            pltpu.SemaphoreType.DMA((3,)),
             *[pltpu.SemaphoreType.DMA((9,))] * 4,
         ],
         compiler_params=pltpu.CompilerParams(
-            collective_id=0, has_side_effects=True, vmem_limit_bytes=62 * 1024 * 1024
+            collective_id=0, has_side_effects=True, vmem_limit_bytes=50 * 1024 * 1024
         ),
         name="hedging",
     )(

time: 88.8 us -> 81.1 us (0.913)
  Pallas kernels: 72.8 us -> 67.9 us
  local copies, waits for them, and re-layouts: 6.43 us -> 3.61 us
    pallas_call x1, Pallas kernels: 72.8 us -> 67.9 us  [per_device(): pl.pallas_call(functools.partial(whole_kernel, chunks, most, ny, nx, nz),...]
    unnamed x9 -> x5, local copies, waits for them, and re-layouts: 6.43 us -> 3.61 us
where the time goes in v3:
time: 81.1 us; the launch traced here: 80.8 us
  Pallas kernels  67.9 us (84%)
  other arithmetic  8.62 us (11%)
  local copies, waits for them, and re-layouts  3.61 us (4%)
    pallas_call x1, Pallas kernels, per_device(): pl.pallas_call(functools.partial(whole_kernel, chunks, most, ny, nx, nz),...  67.9 us
    unnamed x5, local copies, waits for them, and re-layouts  3.61 us

profile of v3, /device:TPU:1, one launch (start us, length us, event | category | flops | bytes accessed | tf_op | source)
XLA Modules:
  0.0 80.8 jit_solution(8829942722540509533)
XLA Ops:
  0.6 1.2 %broadcast_subtract_fusion.local_of = s32[4]{0:T(128)} fusion(s32[4]{0:T(128)} %node_of.1, s32[]{:T(128)S(6)} %mul_shard_map.3), kind=kLoop, calls=%fused_computation.20 | loop fusion | flops 4 | bytes 36 | tf_op jit(solution)/shard_map/sub | solution.py:551
  1.8 0.9 %select_reduce_fusion = s32[512]{0:T(512)S(1)} fusion(s32[512]{0:T(512)} %param.11), kind=kLoop, calls=%fused_computation.4 | loop fusion | flops 785920 | bytes 4096 | tf_op jit(solution)/shard_map/tables/reduce_sum | solution.py:547
  2.7 1.1 %convert_reduce_fusion.2 = s32[512]{0:T(512)S(1)} fusion(s32[512]{0:T(512)} %param.12), kind=kLoop, calls=%fused_computation.9 | loop fusion | flops 1834496 | bytes 4096 | tf_op jit(solution)/shard_map/tables/reduce_sum | solution.py:536
  3.8 1.1 %select_reduce_fusion.1 = (s32[512]{0:T(512)S(1)}, s32[512]{0:T(512)S(1)}) fusion(s32[512]{0:T(512)S(1)} %convert_reduce_fusion.2, s32[512]{0:T(512)} %param.12), kind=kLoop, calls=%fused_computation.6 | loop fusion | flops 1309696 | bytes 8192 | tf_op jit(solution)/shard_map/tables/reduce_sum | solution.py:539
  4.8 0.0 copy-start
  4.8 0.1 slice_compare_fusion
  4.9 0.7 add_convert_fusion.follows
  5.6 0.6 broadcast_multiply_fusion
  6.2 1.3 %broadcast_multiply_fusion.2 = (s32[512]{0:T(512)}, s32[512]{0:T(512)}) fusion(s32[512]{0:T(512)} %param.11, s32[512]{0:T(512)} %param.12), kind=kLoop, calls=%fused_computation.18 | loop fusion | flops 1024 | bytes 8192 | tf_op jit(solution)/shard_map/tables/mul | solution.py:550
  7.4 1.2 %convert_reduce_fusion.1 = (s32[1024]{0:T(1024)S(1)}, s32[1024]{0:T(1024)S(1)}) fusion(s32[512]{0:T(512)} %param.12), kind=kLoop, calls=%fused_computation.2 | loop fusion | flops 3143680 | bytes 10240 | tf_op jit(solution)/shard_map/tables/reduce_sum | solution.py:545
  8.7 0.6 select_multiply_fusion.last4
  9.3 0.0 copy-done
  9.3 67.9 %hedging.1 = (f32[4096,128]{1,0:T(8,128)S(1)}, f32[2048,128]{1,0:T(8,128)S(1)}, f32[4096,128]{1,0:T(8,128)S(1)}) custom-call(s32[512]{0:T(512)} %get-tuple-element.16.cols4, s32[512]{0:T(512)} %get-tuple-element.15.rows4, s32[512]{0:T(512)} %copy-done, s32[512]{0:T(512)} %get-tuple-element.14.order4, f32[512]{0:T(512)} %add_convert_fusion.follows, ...), custom_call_target="tpu_custom_call" | custom-call | tf_op jit(solution)/shard_map/hedging/pallas_call | solution.py:584
  77.2 1.3 %copy.26 = f32[4,131072]{1,0:T(4,128)} copy(f32[4,131072]{1,0:T(4,128)S(1)} %bitcast.29) | data formatting | bytes 4194304
  78.5 1.0 %copy.27 = f32[4,65536]{1,0:T(4,128)} copy(f32[4,65536]{1,0:T(4,128)S(1)} %bitcast.30) | data formatting | bytes 2097152
  79.5 1.3 %copy.28 = f32[4,131072]{1,0:T(4,128)} copy(f32[4,131072]{1,0:T(4,128)S(1)} %bitcast.28) | data formatting | bytes 4194304
Async XLA Ops:
  4.8 4.4 %copy-start = (s32[512]{0:T(512)}, s32[512]{0:T(512)S(1)}, u32[]{:S(2)}) copy-start(s32[512]{0:T(512)S(1)} %get-tuple-element.12.order) | copy-start | bytes 6148

commit v4 on v3

--- a/solution.py
+++ b/solution.py
@@ -243,7 +243,7 @@
 
 class Exchange:
     def __init__(self, ny, nx, nz, bufs, send, recv):
-        (self.root_part, self.node_part, self.r0, self.n0, self.rsum, self.nsum, self.r1, self.n1,
+        (self.root_part, self.node_part, self.n0, self.nsum, self.r1, self.n1,
          self.rz, self.r2, self.root_all, self.node_all) = bufs
         self.send, self.recv = send, recv
         sub, leaf = lax.axis_index("sub"), lax.axis_index("leaf")
@@ -251,17 +251,19 @@
         y, x = leaf // nx, leaf % nx
         self.z, self.core, self.leaf, self.nz = z, core, leaf, nz
         self.cells = ny * nx
-        self.chunk = self.rsum.shape[0] // self.cells
+        self.chunk = self.rz.shape[0]
         self.rows = self.nsum.shape[0] // nz
         self.partner = {"sub": z * 2 + (1 - core), "leaf": leaf}
         self.plane, self.column = [], []
-        for k in range(1, self.cells):
-            other = ((y + k // nx) % ny) * nx + (x + k % nx) % nx
-            self.plane.append((k, other, {"sub": sub, "leaf": other}))
+        for k in range(1, 2 * self.cells):
+            cell = k % self.cells
+            other = ((y + cell // nx) % ny) * nx + (x + cell % nx) % nx
+            half = (core + k // self.cells) % 2
+            self.plane.append((k, half * self.cells + other, {"sub": z * 2 + half, "leaf": other}))
         for k in range(1, nz):
             other = (z + k) % nz
             self.column.append((k, other, {"sub": other * 2 + core, "leaf": leaf}))
-        self.peers = [self.partner] + [p[2] for p in self.plane] + [p[2] for p in self.column]
+        self.peers = [p[2] for p in self.plane] + [p[2] for p in self.column]
 
     def push(self, src, dst, which, peer):
         pltpu.make_async_remote_copy(
@@ -269,24 +271,16 @@
             device_id=peer, device_id_type=MESH,
         ).start()
 
-    def root_to_partner(self):
-        half = self.cells * self.chunk
-        src = self.root_part.at[pl.ds(aligned((1 - self.core) * half), half)]
-        self.push(src, self.r0, 1, self.partner)
-
     def node_to_partner(self):
         half = self.nz * self.rows
         src = self.node_part.at[pl.ds(aligned((1 - self.core) * half), half)]
         self.push(src, self.n0, 0, self.partner)
 
     def root_to_plane(self):
-        half = self.cells * self.chunk
-        wait_bytes(self.r0, self.recv.at[1])
-        self.rsum[...] = self.root_part[pl.ds(aligned(self.core * half), half), :] + self.r0[...]
-        for k, other, peer in self.plane:
+        for k, place, peer in self.plane:
             self.push(
-                self.rsum.at[pl.ds(aligned(other * self.chunk), self.chunk)],
-                self.r1.at[pl.ds((k - 1) * self.chunk, self.chunk)], 3, peer,
+                self.root_part.at[pl.ds(aligned(place * self.chunk), self.chunk)],
+                self.r1.at[pl.ds((k - 1) * self.chunk, self.chunk)], 1, peer,
             )
 
     def node_to_column(self):
@@ -311,9 +305,10 @@
             self.push(self.node_all.at[spot], self.node_all.at[spot], 4, peer)
 
     def root_to_column(self):
-        wait_bytes(self.r1, self.recv.at[3])
-        acc = self.rsum[pl.ds(aligned(self.leaf * self.chunk), self.chunk), :]
-        for k in range(1, self.cells):
+        wait_bytes(self.r1, self.recv.at[1])
+        place = self.core * self.cells + self.leaf
+        acc = self.root_part[pl.ds(aligned(place * self.chunk), self.chunk), :]
+        for k in range(1, 2 * self.cells):
             acc = acc + self.r1[pl.ds((k - 1) * self.chunk, self.chunk), :]
         self.rz[...] = acc
         for k, other, peer in self.column:
@@ -327,8 +322,8 @@
             total = total + self.r2[pl.ds((k - 1) * self.chunk, self.chunk), :]
         spot = pl.ds(aligned((self.core * self.cells + self.leaf) * keep), keep)
         self.root_all[spot, :] = total[:keep] / total[keep:keep + 1]
-        for k, other, peer in self.plane:
-            self.push(self.root_all.at[spot], self.root_all.at[spot], 7, peer)
+        for k, place, peer in self.plane:
+            self.push(self.root_all.at[spot], self.root_all.at[spot], 3, peer)
 
     def node_home(self):
         half = self.nz * (self.rows - 8)
@@ -336,26 +331,19 @@
         spot = self.node_all.at[pl.ds(aligned(self.core * half), half)]
         self.push(spot, spot, 6, self.partner)
 
-    def root_home(self):
+    def finish(self):
         keep = self.chunk - 8
-        half = self.cells * keep
-        wait_bytes(self.root_all.at[pl.ds(0, half - keep)], self.recv.at[7])
-        spot = self.root_all.at[pl.ds(aligned(self.core * half), half)]
-        self.push(spot, spot, 8, self.partner)
-
-    def finish(self):
         wait_bytes(self.node_all.at[pl.ds(0, self.nz * (self.rows - 8))], self.recv.at[6])
-        wait_bytes(self.root_all.at[pl.ds(0, self.cells * (self.chunk - 8))], self.recv.at[8])
+        wait_bytes(self.root_all.at[pl.ds(0, (2 * self.cells - 1) * keep)], self.recv.at[3])
 
     def drain(self):
         width, keep = self.rows - 8, self.chunk - 8
         sent = [
-            self.n0, self.r0, self.n1, self.r1,
+            self.n0, self.r1, self.n1,
+            self.root_all.at[pl.ds(0, (2 * self.cells - 1) * keep)],
             self.node_all.at[pl.ds(0, (self.nz - 1) * width)],
             self.r2,
             self.node_all.at[pl.ds(0, self.nz * width)],
-            self.root_all.at[pl.ds(0, (self.cells - 1) * keep)],
-            self.root_all.at[pl.ds(0, self.cells * keep)],
         ]
         for which, ref in enumerate(sent):
             wait_bytes(ref, self.send.at[which])
@@ -369,10 +357,10 @@
     tiles, field, wide, demand_f, demand_n, dual, sums, second, third, filled, mask, rest,
     total, vals, hot_root, hot_node, *others,
 ):
-    bufs, (sems, send0, recv0, send1, recv1) = others[:24], others[24:]
+    bufs, (sems, send0, recv0, send1, recv1) = others[:20], others[20:]
     rounds = [
-        Exchange(ny, nx, nz, bufs[:12], send0, recv0),
-        Exchange(ny, nx, nz, bufs[12:], send1, recv1),
+        Exchange(ny, nx, nz, bufs[:10], send0, recv0),
+        Exchange(ny, nx, nz, bufs[10:], send1, recv1),
     ]
     start_tiles(tiles_hbm, tiles, sems, chunks)
     barrier = pltpu.get_barrier_semaphore()
@@ -425,10 +413,9 @@
     go = rounds[0]
     weigh_root(second, prob, root_blocks, total, go.root_part)
     pl.semaphore_wait(barrier, len(go.peers))
-    go.root_to_partner()
+    go.root_to_plane()
     weigh_nodes(second, prob, node_of, local_of, node_blocks, vals, go.node_part)
     go.node_to_partner()
-    go.root_to_plane()
     forward((0, 2))
     go.node_to_column()
     forward((2, 8))
@@ -440,7 +427,6 @@
     carry = backward((6, 8), carry)
     mark_blocks(root_row, node_row, node_of, hot_root, hot_node, mask)
     go.node_home()
-    go.root_home()
     go.finish()
 
     def keep_means(at, means):
@@ -469,10 +455,9 @@
 
     go = rounds[1]
     weigh_root(last, prob, root_blocks, total, go.root_part)
-    go.root_to_partner()
+    go.root_to_plane()
     weigh_nodes(last, prob, node_of, local_of, node_blocks, vals, go.node_part)
     go.node_to_partner()
-    go.root_to_plane()
     forward((0, 2))
     go.node_to_column()
     forward((2, 8))
@@ -496,7 +481,6 @@
     loop(rows // 16, 8, rest_body)
     go.root_back()
     go.node_home()
-    go.root_home()
     go.finish()
 
     def update(at, means):
@@ -505,6 +489,70 @@
     fill_means(go.root_all, go.node_all, hot_root, hot_node, local_of, update)
     rounds[0].drain()
     rounds[1].drain()
+
+
+def table_kernel(
+    cols, rows, node_of, cols4, rows4, order, order4, follows, last4, inverse4, local_of
+):
+    nt, nvt, nct = cols.shape[1], last4.shape[1], inverse4.shape[1]
+    local_of[...] = node_of[...] - 8 * lax.axis_index("leaf")
+    cols4[...] = 4 * cols[...]
+    rows4[...] = 4 * rows[...]
+
+    def column(line):
+        return jnp.transpose(jnp.broadcast_to(line.astype(F32), (LANES, nt)))
+
+    def ramp(count, width, start):
+        return (lax.broadcasted_iota(jnp.int32, (count, width), 1) + start).astype(F32)
+
+    def parts(count):
+        width = min(count, LANES)
+        return [(k, width) for k in range(0, count, width)]
+
+    col_c, row_c = column(cols[...]), column(rows[...])
+    n_c = lax.broadcasted_iota(jnp.int32, (nt, LANES), 0).astype(F32)
+    ahead = 0.0
+    for k, width in parts(nt):
+        other = jnp.broadcast_to(cols[:, k:k + width].astype(F32), (nt, width))
+        mine = col_c[:, :width]
+        tie = (other == mine) & (ramp(nt, width, k) < n_c[:, :width])
+        ahead = ahead + ((other < mine) | tie).astype(F32)
+    rank = jnp.dot(
+        ahead.astype(BF16), jnp.ones((ahead.shape[1], LANES), BF16), preferred_element_type=F32
+    )
+    n_r = lax.broadcasted_iota(jnp.int32, (8, nt), 1)
+    col_r = jnp.broadcast_to(cols[...], (8, nt))
+    line = lax.broadcasted_iota(jnp.int32, (8, nt), 0)
+    picks = jnp.where(
+        line == 0, n_r >> 3, jnp.where(line == 1, n_r & 7, jnp.where(line == 2, col_r >> 3, col_r & 7))
+    ).astype(F32).astype(BF16)
+
+    def choose(match):
+        return jnp.dot(picks, match.astype(F32).astype(BF16), preferred_element_type=F32)
+
+    sorted_cols = []
+    for k, width in parts(nt):
+        got = choose(rank[:, :width] == ramp(nt, width, k))
+        place = (8.0 * got[0:1] + got[1:2]).astype(jnp.int32)
+        order[:, k:k + width] = place
+        order4[:, k:k + width] = 4 * place
+        sorted_cols.append(jnp.broadcast_to(8.0 * got[2:3] + got[3:4], (8, width)))
+    here = jnp.concatenate(sorted_cols, axis=1)
+    same = (here == pltpu.roll(here, 1, 1)) & (n_r > 0)
+    follows[...] = same.astype(F32)[0:1]
+    counts = []
+    ones = jnp.ones((8, nt), BF16)
+    for k, width in parts(nvt):
+        upto = (col_c[:, :width] <= ramp(nt, width, k)).astype(F32).astype(BF16)
+        counts.append(jnp.dot(ones, upto, preferred_element_type=F32))
+    upto = jnp.concatenate(counts, axis=1)
+    first = lax.broadcasted_iota(jnp.int32, (8, nvt), 1) == 0
+    before = jnp.where(first, 0.0, pltpu.roll(upto, 1, 1))
+    last = jnp.where(upto > before, upto - 1.0, float(nt))
+    last4[...] = (4.0 * last).astype(jnp.int32)[0:1]
+    for k, width in parts(nct):
+        got = choose(row_c[:, :width] == ramp(nt, width, k))
+        inverse4[:, k:k + width] = (32.0 * got[0:1] + 4.0 * got[1:2]).astype(jnp.int32)
 
 
 def as_rows(field):
@@ -528,27 +576,23 @@
     leaf = lax.axis_size("leaf")
     chunks = 4
     most = 64
-    with jax.named_scope("tables"):
-        n = jnp.arange(nt, dtype=jnp.int32)
-        ahead = (tile_cols[None, :] < tile_cols[:, None]) | (
-            (tile_cols[None, :] == tile_cols[:, None]) & (n[None, :] < n[:, None])
-        )
-        rank = jnp.sum(ahead.astype(jnp.int32), axis=1)
-        place = rank[None, :] == n[:, None]
-        order = jnp.sum(jnp.where(place, n[None, :], 0), axis=1)
-        sorted_col = jnp.sum(jnp.where(place, tile_cols[None, :], 0), axis=1)
-        follows = jnp.concatenate(
-            [jnp.zeros((1,), F32), (sorted_col[1:] == sorted_col[:-1]).astype(F32)]
-        )
-        v = jnp.arange(nvt, dtype=jnp.int32)
-        upto = jnp.sum((tile_cols[None, :] <= v[:, None]).astype(jnp.int32), axis=1)
-        has = jnp.sum((tile_cols[None, :] == v[:, None]).astype(jnp.int32), axis=1)
-        last4 = 4 * jnp.where(has > 0, upto - 1, nt)
-        inverse4 = 4 * jnp.sum(
-            jnp.where(tile_rows[None, :] == jnp.arange(nct)[:, None], n[None, :], 0), axis=1
-        )
-        cols4, rows4, order4 = 4 * tile_cols, 4 * tile_rows, 4 * order
-    local_of = node_of_scen - 8 * lax.axis_index("leaf")
+    vm = pl.BlockSpec(memory_space=pltpu.VMEM)
+
+    def line(count, dtype=jnp.int32):
+        return jax.ShapeDtypeStruct((1, count), dtype)
+
+    tables = pl.pallas_call(
+        table_kernel,
+        out_shape=[
+            line(nt), line(nt), line(nt), line(nt), line(nt, F32), line(nvt), line(nct), line(4),
+        ],
+        in_specs=[vm] * 3,
+        out_specs=[vm] * 8,
+        name="tables",
+    )(tile_cols.reshape(1, nt), tile_rows.reshape(1, nt), node_of_scen.reshape(1, 4))
+    cols4, rows4, order, order4, follows, last4, inverse4, local_of = [
+        table.reshape(-1) for table in tables
+    ]
     cost_r, demand_r = as_rows(cost), as_rows(demand)
     upper_r = upper.reshape(nvt, LANES)
     root_row = root_blocks.reshape(1, root_count)
@@ -561,7 +605,6 @@
     pad_rows = PAD + 4 * nt + 16
     state_rows = 4 * nvt
     sm = pl.BlockSpec(memory_space=pltpu.SMEM)
-    vm = pl.BlockSpec(memory_space=pltpu.VMEM)
     hbm = pl.BlockSpec(memory_space=pl.ANY)
 
     def lines(count):
@@ -570,11 +613,9 @@
     exchange = [
         lines(2 * leaf * chunk),
         lines(8 * node_rows),
-        lines(leaf * chunk),
         lines(nz * node_rows),
-        lines(leaf * chunk),
         lines(nz * node_rows),
-        lines((leaf - 1) * chunk),
+        lines((2 * leaf - 1) * chunk),
         lines((nz - 1) * node_rows),
         lines(chunk),
         lines((nz - 1) * chunk),
@@ -606,7 +647,7 @@
             *exchange,
             *exchange,
             pltpu.SemaphoreType.DMA((chunks,)),
-            *[pltpu.SemaphoreType.DMA((9,))] * 4,
+            *[pltpu.SemaphoreType.DMA((7,))] * 4,
         ],
         compiler_params=pltpu.CompilerParams(
             collective_id=0, has_side_effects=True, vmem_limit_bytes=50 * 1024 * 1024

time: 81.1 us -> 74.4 us (0.917)
  other arithmetic: 8.62 us -> 0 us
  Pallas kernels: 67.9 us -> 70 us
    reduce_sum x4 -> x0, other arithmetic: 4.22 us -> none  [the longest x1 1.23 us: per_device(): has = jnp.sum((tile_cols[None, :] == v[:, None]).astype(jnp.int32), axis=1)]
    mul x3 -> x0, other arithmetic: 2.47 us -> none  [the longest x1 1.28 us: per_device(): cols4, rows4, order4 = (4 * tile_cols, 4 * tile_rows, 4 * order)]
    pallas_call x0 -> x1, Pallas kernels: none -> 2.17 us  [per_device(): pl.pallas_call(table_kernel, out_shape=[line(nt), line(nt), line(nt), lin...]
    sub x1 -> x0, other arithmetic: 1.2 us -> none  [per_device(): local_of = node_of_scen - 8 * lax.axis_index('leaf')]
    unnamed x5 -> x3, local copies, waits for them, and re-layouts: 3.61 us -> 3.61 us
where the time goes in v4:
time: 74.4 us; the launch traced here: 74.2 us
  Pallas kernels  70 us (94%)
  local copies, waits for them, and re-layouts  3.61 us (5%)
    pallas_call x1, Pallas kernels, per_device(): pl.pallas_call(functools.partial(whole_kernel, chunks, most, ny, nx, nz),...  67.8 us
    unnamed x3, local copies, waits for them, and re-layouts  3.61 us
    pallas_call x1, Pallas kernels, per_device(): pl.pallas_call(table_kernel, out_shape=[line(nt), line(nt), line(nt), lin...  2.17 us

profile of v4, /device:TPU:1, one launch (start us, length us, event | category | flops | bytes accessed | tf_op | source)
XLA Modules:
  0.0 74.2 jit_solution(5257453806468631978)
XLA Ops:
  0.6 2.2 %tables.1 = (s32[1,512]{1,0:T(1,128)}, s32[1,512]{1,0:T(1,128)}, s32[1,512]{1,0:T(1,128)}, s32[1,512]{1,0:T(1,128)}, f32[1,512]{1,0:T(1,128)}, /*index=5*/s32[1,...) custom-call(s32[1,512]{1,0:T(1,128)} %bitcast.49, s32[1,512]{1,0:T(1,128)} %bitcast.50, s32[1,4]{1,0:T(1,128)} %bitcast.48), custom_call_target="tpu_custom_call" | custom-call | tf_op jit(solution)/shard_map/tables/pallas_call | solution.py:584
  2.8 67.8 %hedging.1 = (f32[4096,128]{1,0:T(8,128)S(1)}, f32[2048,128]{1,0:T(8,128)S(1)}, f32[4096,128]{1,0:T(8,128)S(1)}) custom-call(s32[512]{0:T(512)} %bitcast.51, s32[512]{0:T(512)} %bitcast.52, s32[512]{0:T(512)} %bitcast.53, s32[512]{0:T(512)} %bitcast.54, f32[512]{0:T(512)} %bitcast.55, s32[1024]{0:T(1024)} %bitcast.47, s32[512]{0:T(512)} %bitcast.56, f32[4]{0:T(128)} %prob.1, ...), custom_call_target="tpu_custom_call" | custom-call | tf_op jit(solution)/shard_map/hedging/pallas_call | solution.py:625
  70.6 1.3 %copy.21 = f32[4,131072]{1,0:T(4,128)} copy(f32[4,131072]{1,0:T(4,128)S(1)} %bitcast.40) | data formatting | bytes 4194304
  72.0 1.0 %copy.22 = f32[4,65536]{1,0:T(4,128)} copy(f32[4,65536]{1,0:T(4,128)S(1)} %bitcast.41) | data formatting | bytes 2097152
  72.9 1.3 %copy.23 = f32[4,131072]{1,0:T(4,128)} copy(f32[4,131072]{1,0:T(4,128)S(1)} %bitcast.39) | data formatting | bytes 4194304
